TPU v7x, 32 devices: a whole 2x2x4 slice. The times are simulated.
32 devices in a mesh: kv: 2 (over x), seq: 16 (over z, y, core).
Axes of the slice: x: 2, y: 2, z: 4, core: 2. Of those that a mesh axis runs over, the one named last changes fastest.
Arguments:
- hidden: bfloat16 [1024, 2048], P('seq', 'kv'), may hold values from -1.5 to 1.5
- in_gain: float32 [2048], replicated, may hold values from 0.5 to 1.5
- w_query: bfloat16 [2048, 2048], P(None, 'kv'), may hold values from -0.125 to 0.125
- key_projection_weight: bfloat16 [2048, 1024], P(None, 'kv'), may hold values from -0.125 to 0.125
- value_projection_weight: bfloat16 [2048, 1024], P(None, 'kv'), may hold values from -0.125 to 0.125
- w_gate: bfloat16 [2048, 16], P(None, 'kv'), may hold values from -0.125 to 0.125
- w_out: bfloat16 [2048, 2048], P('kv'), may hold values from -0.125 to 0.125
- q_gain: float32 [128], replicated, may hold values from 0.1 to 1.9
- k_gain: float32 [128], replicated, may hold values from 0.1 to 1.9
- cache_keys: bfloat16 [32768, 8, 128], P('seq', 'kv'), may hold values from -160 to 160
- pooled_cache_values: bfloat16 [32768, 8, 128], P('seq', 'kv'), may hold values from -6 to 6
- prefix_len: int32 [4], replicated, may hold values from 1024 to 8192, as said below
- own_len: int32 [32], replicated, may hold values from 256 to 2048, as said below
- request_group: int32 [32], replicated, may hold values from 0 to 3, as said below
- parents: int32 [32, 32], P('seq'), may hold values from 0 to 30, as said below
- accepted_leaf: int32 [32], P('seq'), may hold values from 0 to 31
Outputs:
- layer_out: bfloat16 [1024, 2048], P('seq', 'kv')
- accepted_keys: bfloat16 [32, 32, 1024], P('seq', None, 'kv')
- accepted_values: bfloat16 [32, 32, 1024], P('seq', None, 'kv')
Inputs may be any that keep to these rules, and one draw needn't show every extreme that they name: parents[r, 0] is 0 and node 0 is the root; for i >= 1, parents[r, i] < i. `prefix_len`: the lengths sum to 32768 // 2; one is exactly 8192 and one exactly 1024. `own_len`: the lengths sum to 32768 // 2; one is exactly 2048 and one exactly 256. `request_group`: every group holds exactly 8 requests.
All inputs are finite; a program needn't handle non-finite values.
Results may differ from a plain program's by a relative error of at most 0.017.
The roundings to bfloat16 on the way count: a program that leaves them out, or rounds other values in their place, can miss the bound.
Values may be sent and summed in bfloat16 or wider, within the bound.
A program may use at most 128 MiB of HBM per device.

v0:
```python
import math

import jax
import jax.numpy as jnp
from jax import lax
from jax.sharding import PartitionSpec as P

EPSILON = 1e-06
ROPE_BASE = 1000000.0
NEGATIVE = -1e30


def rms_scale(values, scales):
    mean_square = jnp.mean(values * values, axis=-1, keepdims=True)
    return values * lax.rsqrt(mean_square + EPSILON) * scales


def rotate_pairs(values, positions):
    half_width = values.shape[-1] // 2
    freqs = jnp.exp(
        jnp.arange(half_width, dtype=jnp.float32) * (-2.0 * math.log(ROPE_BASE) / values.shape[-1])
    )
    angles = positions[:, None] * freqs[None, :]
    cosine = jnp.concatenate([jnp.cos(angles), jnp.cos(angles)], axis=-1)[:, None, :]
    sine = jnp.concatenate([jnp.sin(angles), jnp.sin(angles)], axis=-1)[:, None, :]
    turned = jnp.concatenate([-values[..., half_width:], values[..., :half_width]], axis=-1)
    return values * cosine + turned * sine


def tree_paths(parents):
    width = parents.shape[-1]
    nodes = jnp.arange(width, dtype=jnp.int32)
    linked = (parents[:, :, None] == nodes[None, None, :]).astype(jnp.float32)
    identity_mat = jnp.eye(width, dtype=jnp.float32)
    reach = jnp.minimum(identity_mat[None] + linked * (1.0 - identity_mat[None]), 1.0)
    for squaring in range(max(1, (width - 1).bit_length())):
        reach = jnp.minimum(
            jnp.einsum("mij,mjk->mik", reach, reach, precision=lax.Precision.HIGHEST), 1.0
        )
    depth_f = jnp.sum(reach, axis=-1) - 1.0
    return (reach, depth_f)


def accepted_rows(reach, depth_f, leaves, tree_rows):
    width = reach.shape[-1]
    nodes = jnp.arange(width, dtype=jnp.int32)
    leaf_pick = (leaves[:, None] == nodes[None, :]).astype(jnp.float32)
    on_path = jnp.einsum("mi,mij->mj", leaf_pick, reach, precision=lax.Precision.HIGHEST)
    levels = (depth_f[:, None, :] == nodes.astype(jnp.float32)[None, :, None]).astype(jnp.float32)
    select = levels * on_path[:, None, :]
    return jnp.einsum(
        "mdj,mjc->mdc", select, tree_rows.astype(jnp.float32), precision=lax.Precision.HIGHEST
    ).astype(jnp.bfloat16)


def body(
    hidden,
    in_gain,
    w_query,
    key_projection_weight,
    value_projection_weight,
    w_gate,
    w_out,
    q_gain,
    k_gain,
    cache_keys,
    pooled_cache_values,
    prefix_len,
    own_len,
    request_group,
    parents,
    accepted_leaf,
):
    local_req, tree = parents.shape
    groups = prefix_len.shape[0]
    requests = own_len.shape[0]
    head_width = q_gain.shape[0]
    local_heads = w_gate.shape[1]
    local_kv = key_projection_weight.shape[1] // head_width
    per_kv = local_heads // local_kv
    local_tok = hidden.shape[0]
    pool_dev = cache_keys.shape[0]
    seq_index = lax.axis_index("seq")
    score_scale = 1.0 / math.sqrt(head_width)
    full_rows = lax.all_gather(hidden, "kv", axis=1, tiled=True)
    normed = rms_scale(full_rows.astype(jnp.float32), in_gain).astype(jnp.bfloat16)
    reach, depth_f = tree_paths(parents)
    all_reqs = jnp.arange(requests, dtype=jnp.int32)
    my_reqs = seq_index * local_req + jnp.arange(local_req, dtype=jnp.int32)
    my_pick = (my_reqs[:, None] == all_reqs[None, :]).astype(jnp.int32)
    my_group = jnp.sum(my_pick * request_group[None, :], axis=1)
    group_ids = jnp.arange(groups, dtype=jnp.int32)
    group_pick = (my_group[:, None] == group_ids[None, :]).astype(jnp.int32)
    context = jnp.sum(group_pick * prefix_len[None, :], axis=1) + jnp.sum(
        my_pick * own_len[None, :], axis=1
    )
    positions = (context[:, None].astype(jnp.float32) + depth_f).reshape(-1)
    query = jnp.dot(normed, w_query, preferred_element_type=jnp.float32).reshape(
        local_tok, local_heads, head_width
    )
    query = rotate_pairs(rms_scale(query, q_gain), positions).astype(jnp.bfloat16)
    key_new = jnp.dot(normed, key_projection_weight, preferred_element_type=jnp.float32).reshape(
        local_tok, local_kv, head_width
    )
    key_new = rotate_pairs(rms_scale(key_new, k_gain), positions).astype(jnp.bfloat16)
    value_new = (
        jnp.dot(normed, value_projection_weight, preferred_element_type=jnp.float32)
        .astype(jnp.bfloat16)
        .reshape(local_tok, local_kv, head_width)
    )
    gate_logit = jnp.dot(normed, w_gate, preferred_element_type=jnp.float32)
    tree_query = query.reshape(local_req, tree, local_kv, per_kv, head_width)
    tree_keys = key_new.reshape(local_req, tree, local_kv, head_width)
    tree_values = value_new.reshape(local_req, tree, local_kv, head_width)
    tree_scores = (
        jnp.einsum("atkgd,askd->atkgs", tree_query, tree_keys, preferred_element_type=jnp.float32)
        * score_scale
    )
    tree_seen = (reach > 0.5)[:, :, None, None, :]
    tree_scores = jnp.where(tree_seen, tree_scores, NEGATIVE)
    tree_max = jnp.max(tree_scores, axis=-1)
    tree_weights = jnp.where(tree_seen, jnp.exp(tree_scores - tree_max[..., None]), 0.0)
    tree_sum = jnp.sum(tree_weights, axis=-1).reshape(local_tok, local_heads)
    tree_num = jnp.einsum(
        "atkgs,askd->atkgd",
        tree_weights.astype(jnp.bfloat16),
        tree_values,
        preferred_element_type=jnp.float32,
    ).reshape(local_tok, local_heads, head_width)
    tree_max = tree_max.reshape(local_tok, local_heads)
    lengths_all = jnp.concatenate([prefix_len, own_len])
    starts = jnp.cumsum(lengths_all) - lengths_all
    slot_ids = seq_index * pool_dev + jnp.arange(pool_dev, dtype=jnp.int32)
    slot_segment = jnp.sum((starts[None, :] <= slot_ids[:, None]).astype(jnp.int32), axis=1) - 1
    block_len = min(512, pool_dev)
    block_count = pool_dev // block_len
    key_blocks = cache_keys.reshape(block_count, block_len, local_kv, head_width)
    value_blocks = pooled_cache_values.reshape(block_count, block_len, local_kv, head_width)
    segment_blocks = slot_segment.reshape(block_count, block_len)
    query_flat = query.reshape(local_tok, local_heads * head_width)
    query_piece = lax.all_gather(query_flat, "seq", axis=0, tiled=True)
    row_ids = jnp.arange(query_piece.shape[0], dtype=jnp.int32)
    owners = row_ids // tree
    count = query_piece.shape[0]
    grouped = query_piece.reshape(count, local_kv, per_kv, head_width)
    owner_pick = (owners[:, None] == all_reqs[None, :]).astype(jnp.int32)
    known = owners >= 0
    prefix_segment = jnp.where(known, jnp.sum(owner_pick * request_group[None, :], axis=1), -5)
    own_segment = jnp.where(known, owners + groups, -5)

    def visit(carry, block):
        run_max, run_sum, run_num = carry
        keys_block, values_block, segment_block = block
        scores = (
            jnp.einsum("nkgd,pkd->nkgp", grouped, keys_block, preferred_element_type=jnp.float32)
            * score_scale
        )
        visible = (segment_block[None, :] == prefix_segment[:, None]) | (
            segment_block[None, :] == own_segment[:, None]
        )
        visible = visible[:, None, None, :]
        scores = jnp.where(visible, scores, NEGATIVE)
        new_max = jnp.maximum(run_max, jnp.max(scores, axis=-1))
        weights = jnp.where(visible, jnp.exp(scores - new_max[..., None]), 0.0)
        factor = jnp.exp(run_max - new_max)
        run_sum = run_sum * factor + jnp.sum(weights, axis=-1)
        run_num = run_num * factor[..., None] + jnp.einsum(
            "nkgp,pkd->nkgd",
            weights.astype(jnp.bfloat16),
            values_block,
            preferred_element_type=jnp.float32,
        )
        return ((new_max, run_sum, run_num), None)

    start_state = (
        jnp.full((count, local_kv, per_kv), NEGATIVE, jnp.float32),
        jnp.zeros((count, local_kv, per_kv), jnp.float32),
        jnp.zeros((count, local_kv, per_kv, head_width), jnp.float32),
    )
    final_state, unused = lax.scan(visit, start_state, (key_blocks, value_blocks, segment_blocks))
    run_max, run_sum, run_num = final_state
    part_max = run_max.reshape(count, local_heads)
    part_sum = run_sum.reshape(count, local_heads)
    part_num = run_num.reshape(count, local_heads * head_width)
    all_rows = part_max.shape[0]
    cache_max = lax.pmax(part_max.astype(jnp.bfloat16), "seq").astype(part_max.dtype)
    factor = jnp.exp(part_max - cache_max)
    scaled_num = (part_num.reshape(all_rows, local_heads, head_width) * factor[..., None]).reshape(
        all_rows, local_heads * head_width
    )
    summed_num, summed_sum = (
        lax.psum_scatter(
            scaled_num.astype(jnp.bfloat16), "seq", scatter_dimension=0, tiled=True
        ).astype(jnp.float32),
        lax.psum_scatter(
            (part_sum * factor).astype(jnp.bfloat16), "seq", scatter_dimension=0, tiled=True
        ).astype(jnp.float32),
    )
    own_max = lax.dynamic_slice_in_dim(cache_max, seq_index * local_tok, local_tok, 0)
    final_max = jnp.maximum(own_max, tree_max)
    cache_factor = jnp.exp(own_max - final_max)
    tree_factor = jnp.exp(tree_max - final_max)
    weight_sum = summed_sum * cache_factor + tree_sum * tree_factor
    mixed = (
        summed_num.reshape(local_tok, local_heads, head_width) * cache_factor[..., None]
        + tree_num * tree_factor[..., None]
    )
    mixed = mixed / weight_sum[..., None]
    attended = (
        (mixed * jax.nn.sigmoid(gate_logit)[..., None])
        .astype(jnp.bfloat16)
        .reshape(local_tok, local_heads * head_width)
    )
    projected = jnp.dot(attended, w_out, preferred_element_type=jnp.float32)
    layer_part = lax.psum_scatter(
        projected.astype(jnp.bfloat16), "kv", scatter_dimension=1, tiled=True
    ).astype(jnp.float32)
    layer_out = (layer_part + hidden.astype(jnp.float32)).astype(jnp.bfloat16)
    tree_rows = jnp.concatenate(
        [
            key_new.reshape(local_req, tree, local_kv * head_width),
            value_new.reshape(local_req, tree, local_kv * head_width),
        ],
        axis=-1,
    )
    picked = accepted_rows(reach, depth_f, accepted_leaf, tree_rows)
    accepted_keys = picked[:, :, : local_kv * head_width]
    accepted_values = picked[:, :, local_kv * head_width :]
    return (layer_out, accepted_keys, accepted_values)


def solution(mesh):
    in_specs = (
        P("seq", "kv"),
        P(),
        P(None, "kv"),
        P(None, "kv"),
        P(None, "kv"),
        P(None, "kv"),
        P("kv", None),
        P(),
        P(),
        P("seq", "kv", None),
        P("seq", "kv", None),
        P(),
        P(),
        P(),
        P("seq", None),
        P("seq"),
    )
    out_specs = (P("seq", "kv"), P("seq", None, "kv"), P("seq", None, "kv"))
    return jax.shard_map(body, mesh=mesh, in_specs=in_specs, out_specs=out_specs, check_vma=False)
```

profile of v0, /device:TPU:0, one launch (start us, length us, event | category | flops | bytes accessed | tf_op | source)
XLA Modules:
  0.0 365.4 jit_solution(637547949621892404)
XLA Ops:
  7.3 0.8 broadcast_bitcast_fusion
  8.1 7.4 %all_gather.6 = bf16[64,2048]{1,0:T(8,128)(2,1)S(1)} all-gather(bf16[64,1024]{1,0:T(8,128)(2,1)} %param.18), channel_id=1, replica_groups=mesh['kv'=2,'seq'=16] {'kv'}, dimensions={1}, use_global_device_ids=true | all-gather | bytes 393216 | tf_op jit(solution)/shard_map/all_gather | solution.py:85
  15.6 3.1 fusion.96
  22.7 0.8 fusion.35
  25.8 0.9 fusion.28
  26.7 39.9 %all-gather.2.cloned.1.call-done = bf16[1024,1024]{1,0:T(8,128)(2,1)} async-done(((bf16[64,1024]{1,0:T(8,128)(2,1)}), bf16[1024,1024]{1,0:T(8,128)(2,1)}) %all-gather.2.cloned.1.call-update) | async-done | bytes 2097168 | tf_op jit(solution)/shard_map/all_gather | solution.py:141
  66.6 4.5 %reshape.343 = bf16[1024,4,2,128]{3,2,1,0:T(2,128)(2,1)} reshape(bf16[1024,1024]{1,0:T(8,128)(2,1)} %all-gather.2.cloned.1.call-done) | data formatting | bytes 4194304 | tf_op jit(solution)/shard_map/reshape | solution.py:145
  71.1 3.2 copy.172
  74.3 84.1 %while.15 = (s32[]{:T(128)}, f32[1024,4,2]{0,2,1:T(2,128)S(1)}, f32[1024,4,2]{0,2,1:T(2,128)S(1)}, f32[1024,4,2,128]{0,3,2,1:T(8,128)}, s32[4,512]{1,0:T(4,128)S...) while((s32[]{:T(128)}, f32[1024,4,2]{0,2,1:T(2,128)S(1)}, ...), condition=%wide.region_12.13_spmd.clone, body=%wide.region_9.12_spmd.clone.sunk | while | flops 2206780416 | bytes 69748896 | solution.py:180
  74.7 2.4 constant_dynamic-slice_fusion.6
  77.1 1.1 copy.285
  78.2 4.6 %fusion.137 = (f32[1024,4,2]{0,2,1:T(2,128)S(1)}, f32[4,512,1024,2]{2,1,3,0:T(8,128)S(1)}) fusion(pred[1024,512]{0,1:T(8,128)(4,1)S(1)} %compare_or_fusion.2, bf16[1024,4,2,128]{3,0,2,1:T(8,128)(2,1)} %get-tuple-element.291, bf16[1,512,4,128]{3,2,1,0:T(4,128)(2,1)} %get-tuple-element.256), kind=kOutput, calls=%fused_computation.3.clone.1 | convolution fusion | flops 1086316544 | bytes 19955712 | tf_op jit(solution)/shard_map/while/body/eval_jaxpr/nkgd,pkd->nkgp/dot_general | solution.py:155
  82.8 4.1 %fusion.139 = f32[1024,4,2]{0,2,1:T(2,128)S(1)} fusion(f32[4,512,1024,2]{2,1,3,0:T(8,128)S(1)} %get-tuple-element.258, f32[1024,4,2]{0,2,1:T(2,128)S(1)} %fusion.138, pred[1024,512]{0,1:T(8,128)(4,1)S(1)} %compare_or_fusion.2), kind=kLoop, calls=%fused_computation.5.clone.1 | loop fusion | flops 20963328 | bytes 17367040 | tf_op jit(solution)/shard_map/while/body/eval_jaxpr/reduce_sum | solution.py:166
  87.0 7.1 %bitcast_add_fusion.2 = f32[1024,4,2,128]{0,3,2,1:T(8,128)} fusion(f32[1024,4,2,128]{0,3,2,1:T(8,128)} %get-tuple-element.276, f32[4,512,1024,2]{2,1,3,0:T(8,128)S(1)} %get-tuple-element.258, f32[1024,4,2]{0,2,1:T(2,128)S(1)} %fusion.138, pred[1024,512]{0,1:T(8,128)(4,1)S(1)} %compare_or_fusion.2, f32[1024,4,2]{0,2,1:T(2,128)S(1)} %get-tuple-element.260, ...), kind=kOutput, calls=%fused_computation.8.clone.1 | convolution fusion | flops 1097859072 | bytes 26279936 | tf_op jit(solution)/shard_map/while/body/eval_jaxpr/nkgp,pkd->nkgd/dot_general | solution.py:167
  94.6 2.4 constant_dynamic-slice_fusion.6
  96.9 1.1 copy.285
  98.1 4.6 %fusion.137 = (f32[1024,4,2]{0,2,1:T(2,128)S(1)}, f32[4,512,1024,2]{2,1,3,0:T(8,128)S(1)}) fusion(pred[1024,512]{0,1:T(8,128)(4,1)S(1)} %compare_or_fusion.2, bf16[1024,4,2,128]{3,0,2,1:T(8,128)(2,1)} %get-tuple-element.291, bf16[1,512,4,128]{3,2,1,0:T(4,128)(2,1)} %get-tuple-element.256), kind=kOutput, calls=%fused_computation.3.clone.1 | convolution fusion | flops 1086316544 | bytes 19955712 | tf_op jit(solution)/shard_map/while/body/eval_jaxpr/nkgd,pkd->nkgp/dot_general | solution.py:155
  102.7 4.1 %fusion.139 = f32[1024,4,2]{0,2,1:T(2,128)S(1)} fusion(f32[4,512,1024,2]{2,1,3,0:T(8,128)S(1)} %get-tuple-element.258, f32[1024,4,2]{0,2,1:T(2,128)S(1)} %fusion.138, pred[1024,512]{0,1:T(8,128)(4,1)S(1)} %compare_or_fusion.2), kind=kLoop, calls=%fused_computation.5.clone.1 | loop fusion | flops 20963328 | bytes 17367040 | tf_op jit(solution)/shard_map/while/body/eval_jaxpr/reduce_sum | solution.py:166
  106.9 8.7 %bitcast_add_fusion.2 = f32[1024,4,2,128]{0,3,2,1:T(8,128)} fusion(f32[1024,4,2,128]{0,3,2,1:T(8,128)} %get-tuple-element.276, f32[4,512,1024,2]{2,1,3,0:T(8,128)S(1)} %get-tuple-element.258, f32[1024,4,2]{0,2,1:T(2,128)S(1)} %fusion.138, pred[1024,512]{0,1:T(8,128)(4,1)S(1)} %compare_or_fusion.2, f32[1024,4,2]{0,2,1:T(2,128)S(1)} %get-tuple-element.260, ...), kind=kOutput, calls=%fused_computation.8.clone.1 | convolution fusion | flops 1097859072 | bytes 26279936 | tf_op jit(solution)/shard_map/while/body/eval_jaxpr/nkgp,pkd->nkgd/dot_general | solution.py:167
  116.0 2.4 constant_dynamic-slice_fusion.6
  118.4 1.1 copy.285
  119.5 4.6 %fusion.137 = (f32[1024,4,2]{0,2,1:T(2,128)S(1)}, f32[4,512,1024,2]{2,1,3,0:T(8,128)S(1)}) fusion(pred[1024,512]{0,1:T(8,128)(4,1)S(1)} %compare_or_fusion.2, bf16[1024,4,2,128]{3,0,2,1:T(8,128)(2,1)} %get-tuple-element.291, bf16[1,512,4,128]{3,2,1,0:T(4,128)(2,1)} %get-tuple-element.256), kind=kOutput, calls=%fused_computation.3.clone.1 | convolution fusion | flops 1086316544 | bytes 19955712 | tf_op jit(solution)/shard_map/while/body/eval_jaxpr/nkgd,pkd->nkgp/dot_general | solution.py:155
  124.1 4.1 %fusion.139 = f32[1024,4,2]{0,2,1:T(2,128)S(1)} fusion(f32[4,512,1024,2]{2,1,3,0:T(8,128)S(1)} %get-tuple-element.258, f32[1024,4,2]{0,2,1:T(2,128)S(1)} %fusion.138, pred[1024,512]{0,1:T(8,128)(4,1)S(1)} %compare_or_fusion.2), kind=kLoop, calls=%fused_computation.5.clone.1 | loop fusion | flops 20963328 | bytes 17367040 | tf_op jit(solution)/shard_map/while/body/eval_jaxpr/reduce_sum | solution.py:166
  128.3 8.7 %bitcast_add_fusion.2 = f32[1024,4,2,128]{0,3,2,1:T(8,128)} fusion(f32[1024,4,2,128]{0,3,2,1:T(8,128)} %get-tuple-element.276, f32[4,512,1024,2]{2,1,3,0:T(8,128)S(1)} %get-tuple-element.258, f32[1024,4,2]{0,2,1:T(2,128)S(1)} %fusion.138, pred[1024,512]{0,1:T(8,128)(4,1)S(1)} %compare_or_fusion.2, f32[1024,4,2]{0,2,1:T(2,128)S(1)} %get-tuple-element.260, ...), kind=kOutput, calls=%fused_computation.8.clone.1 | convolution fusion | flops 1097859072 | bytes 26279936 | tf_op jit(solution)/shard_map/while/body/eval_jaxpr/nkgp,pkd->nkgd/dot_general | solution.py:167
  137.4 2.4 constant_dynamic-slice_fusion.6
  139.8 1.1 copy.285
  140.9 4.6 %fusion.137 = (f32[1024,4,2]{0,2,1:T(2,128)S(1)}, f32[4,512,1024,2]{2,1,3,0:T(8,128)S(1)}) fusion(pred[1024,512]{0,1:T(8,128)(4,1)S(1)} %compare_or_fusion.2, bf16[1024,4,2,128]{3,0,2,1:T(8,128)(2,1)} %get-tuple-element.291, bf16[1,512,4,128]{3,2,1,0:T(4,128)(2,1)} %get-tuple-element.256), kind=kOutput, calls=%fused_computation.3.clone.1 | convolution fusion | flops 1086316544 | bytes 19955712 | tf_op jit(solution)/shard_map/while/body/eval_jaxpr/nkgd,pkd->nkgp/dot_general | solution.py:155
  145.5 4.1 %fusion.139 = f32[1024,4,2]{0,2,1:T(2,128)S(1)} fusion(f32[4,512,1024,2]{2,1,3,0:T(8,128)S(1)} %get-tuple-element.258, f32[1024,4,2]{0,2,1:T(2,128)S(1)} %fusion.138, pred[1024,512]{0,1:T(8,128)(4,1)S(1)} %compare_or_fusion.2), kind=kLoop, calls=%fused_computation.5.clone.1 | loop fusion | flops 20963328 | bytes 17367040 | tf_op jit(solution)/shard_map/while/body/eval_jaxpr/reduce_sum | solution.py:166
  149.7 8.7 %bitcast_add_fusion.2 = f32[1024,4,2,128]{0,3,2,1:T(8,128)} fusion(f32[1024,4,2,128]{0,3,2,1:T(8,128)} %get-tuple-element.276, f32[4,512,1024,2]{2,1,3,0:T(8,128)S(1)} %get-tuple-element.258, f32[1024,4,2]{0,2,1:T(2,128)S(1)} %fusion.138, pred[1024,512]{0,1:T(8,128)(4,1)S(1)} %compare_or_fusion.2, f32[1024,4,2]{0,2,1:T(2,128)S(1)} %get-tuple-element.260, ...), kind=kOutput, calls=%fused_computation.8.clone.1 | convolution fusion | flops 1097859072 | bytes 26279936 | tf_op jit(solution)/shard_map/while/body/eval_jaxpr/nkgp,pkd->nkgd/dot_general | solution.py:167
  158.4 5.4 %copy.208 = f32[1024,1024]{1,0:T(8,128)} copy(f32[1024,1024]{0,1:T(8,128)} %bitcast.172) | data formatting | bytes 8388608 | tf_op jit(solution)/shard_map/reshape;reshape | solution.py:188
  163.8 59.5 %pmax.7 = bf16[1024,8]{0,1:T(8,128)(2,1)S(1)} all-reduce(bf16[1024,8]{0,1:T(8,128)(2,1)S(1)} %convert_element_type.109), channel_id=1, replica_groups=mesh['kv'=2,'seq'=16] {'seq'}, use_global_device_ids=true, to_apply=%region_13.14 | all-reduce | flops 8192 | bytes 32768 | tf_op jit(solution)/shard_map/pmax | solution.py:186
  223.3 0.9 copy.213
  224.7 1.1 mul.385
  225.8 1.0 copy-done.1
  226.9 2.2 fusion.23
  229.1 0.7 rsqrt.35
  229.8 0.7 copy.220
  230.5 0.7 reshape.346
  231.2 0.7 rsqrt.36
  232.1 1.4 copy.176
  233.5 0.8 mul.436
  234.2 0.7 mul.437
  234.9 1.4 copy.191
  236.3 2.1 convolution_convert_fusion.2
  239.1 0.9 mul.399.clone
  240.0 0.7 mul.430
  240.7 0.8 fusion.47
  241.9 0.7 mul.441
  242.6 0.8 multiply_cosine_fusion
  243.5 1.4 fusion.102
  245.6 1.1 convolution_bitcast_fusion
  247.1 0.8 fusion.43
  248.0 0.7 compare_bitcast_fusion
  248.7 0.7 broadcast_bitcast_fusion.1
  249.4 0.9 fusion.82
  250.3 1.1 add_convert_fusion.1
  251.4 25.6 %reduce-scatter.10.cloned.1.call-done = bf16[64,8]{1,0:T(8,128)(2,1)} async-done(((bf16[1024,8]{1,0:T(8,128)(2,1)}), bf16[64,8]{1,0:T(8,128)(2,1)}) %reduce-scatter.10.cloned.1.call-update) | async-done | bytes 1040
  277.0 0.8 copy.214
  278.1 63.2 %reduce-scatter.6.cloned.1.call-done = bf16[64,1024]{1,0:T(8,128)(2,1)} async-done(((bf16[1024,1024]{1,0:T(8,128)(2,1)}), bf16[64,1024]{1,0:T(8,128)(2,1)}) %reduce-scatter.6.cloned.1.call-update) | async-done | bytes 131088 | tf_op jit(solution)/shard_map/reduce_scatter | solution.py:192
  341.3 0.9 mul.425
  342.6 3.9 %convolution_convert_fusion = bf16[64,2048]{1,0:T(8,128)(2,1)} fusion(bf16[1024,2048]{1,0:T(8,128)(2,1)} %param.24, f32[8,8,8,128]{3,2,1,0:T(8,128)S(1)} %bitcast.180, f32[8,8,8,128]{3,2,1,0:T(8,128)S(1)} %bitcast.183, f32[64,1024]{1,0:T(8,128)S(1)} %reshape.350, f32[8,8,8,128]{3,2,1,0:T(8,128)S(1)} %bitcast.181, f32[8,8,8,128]{3,2,1,0:T(8,128)S(1)} %bitcast.182, ...), kind=kOutput, calls=%fused_computation.37 | convolution fusion | flops 269025280 | bytes 5898240 | tf_op jit(solution)/shard_map/dot_general | solution.py:214
  346.8 0.7 fusion.100
  347.5 9.8 %reduce-scatter.8.cloned.1.call-done = bf16[64,1024]{1,0:T(8,128)(2,1)} async-done(((bf16[64,2048]{1,0:T(8,128)(2,1)}), bf16[64,1024]{1,0:T(8,128)(2,1)}) %reduce-scatter.8.cloned.1.call-update) | async-done | bytes 131088 | tf_op jit(solution)/shard_map/reduce_scatter | solution.py:215
  357.3 1.6 add_convert_fusion
  (175 shorter events, 12.3 us)
Async XLA Ops:
  7.2 17.1 %copy-start = (bf16[2048,512]{1,0:T(8,128)(2,1)S(1)}, bf16[2048,512]{1,0:T(8,128)(2,1)}, u32[]{:S(2)}) copy-start(bf16[2048,512]{1,0:T(8,128)(2,1)} %param.21) | copy-start | bytes 6291460
  7.2 11.9 %copy-start.21 = (f32[128]{0:T(128)S(1)}, f32[128]{0:T(128)}, u32[]{:S(2)}) copy-start(f32[128]{0:T(128)} %param.25) | copy-start | bytes 1540
  7.2 12.1 %copy-start.28 = (s32[2,32]{1,0:T(2,128)S(1)}, s32[2,32]{1,0:T(2,128)}, u32[]{:S(2)}) copy-start(s32[2,32]{1,0:T(2,128)} %param.32) | copy-start | bytes 772
  7.2 13.1 %copy-start.27 = (s32[32]{0:T(128)S(1)}, s32[32]{0:T(128)}, u32[]{:S(2)}) copy-start(s32[32]{0:T(128)} %param.30) | copy-start | bytes 388
  7.2 13.1 %copy-start.26 = (s32[32]{0:T(128)S(1)}, s32[32]{0:T(128)}, u32[]{:S(2)}) copy-start(s32[32]{0:T(128)} %param.31) | copy-start | bytes 388
  7.2 13.3 %copy-start.29 = (s32[4]{0:T(128)S(1)}, s32[4]{0:T(128)}, u32[]{:S(2)}) copy-start(s32[4]{0:T(128)} %param.29) | copy-start | bytes 52
  7.2 59.4 %all-gather.2.cloned.1.call-start = ((), (), s32[]{:S(2)}) async-start(), calls=%async_computation.3 | async-start | bytes 2228224 | tf_op jit(solution)/shard_map/all_gather | solution.py:141
  7.3 14.6 %copy-start.25 = (f32[64]{0:T(128)}, f32[64]{0:T(128)S(1)}, u32[]{:S(2)}) copy-start(f32[64]{0:T(128)S(1)} %multiply_exponential_fusion) | copy-start | bytes 772
  15.5 10.3 %copy-start.3 = (bf16[64,2048]{1,0:T(8,128)(2,1)}, bf16[64,2048]{1,0:T(8,128)(2,1)S(1)}, u32[]{:S(2)}) copy-start(bf16[64,2048]{1,0:T(8,128)(2,1)S(1)} %all_gather.6) | copy-start | bytes 786436
  15.6 10.2 %copy-start.22 = (f32[64]{0:T(128)}, f32[64]{0:T(128)S(1)}, u32[]{:S(2)}) copy-start(f32[64]{0:T(128)S(1)} %add_rsqrt_fusion.2) | copy-start | bytes 772
  15.6 8.6 %copy-start.19 = (f32[2048]{0:T(1024)S(1)}, f32[2048]{0:T(1024)}, u32[]{:S(2)}) copy-start(f32[2048]{0:T(1024)} %param.19) | copy-start | bytes 24580
  18.8 7.1 %copy-start.30 = (bf16[2048,8]{0,1:T(8,128)(2,1)S(1)}, bf16[2048,8]{0,1:T(8,128)(2,1)}, u32[]{:S(2)}) copy-start(bf16[2048,8]{0,1:T(8,128)(2,1)} %param.23) | copy-start | bytes 98308
  20.3 50.7 %copy-start.15 = (f32[2,32,32]{2,1,0:T(8,128)}, f32[2,32,32]{2,1,0:T(8,128)S(1)}, u32[]{:S(2)}) copy-start(f32[2,32,32]{2,1,0:T(8,128)S(1)} %get-tuple-element.190) | copy-start | bytes 24580
  21.3 49.8 %copy-start.24 = (f32[2,32]{1,0:T(2,128)}, f32[2,32]{1,0:T(2,128)S(1)}, u32[]{:S(2)}) copy-start(f32[2,32]{1,0:T(2,128)S(1)} %get-tuple-element.186) | copy-start | bytes 772
  21.7 0.8 copy-start.16
  21.7 0.6 copy-start.14
  21.9 0.7 copy-start.7
  21.9 0.8 copy-start.9
  23.6 253.4 %reduce-scatter.10.cloned.1.call-start = ((), (), s32[]{:S(2)}) async-start(), calls=%async_computation.6 | async-start | bytes 278528
  24.8 49.5 %copy-start.5 = (f32[64,512]{1,0:T(8,128)}, f32[64,512]{1,0:T(8,128)S(1)}, u32[]{:S(2)}) copy-start(f32[64,512]{1,0:T(8,128)S(1)} %fusion.94) | copy-start | bytes 393220
  82.8 4.2 %copy-start.2 = (bf16[1,512,4,128]{1,3,2,0:T(8,128)(2,1)S(1)}, bf16[1,512,4,128]{1,3,2,0:T(8,128)(2,1)}, u32[]{:S(2)}) copy-start(bf16[1,512,4,128]{1,3,2,0:T(8,128)(2,1)} %copy.285) | copy-start | bytes 1572868 | tf_op jit(solution)/shard_map/while
  102.7 4.2 %copy-start.2 = (bf16[1,512,4,128]{1,3,2,0:T(8,128)(2,1)S(1)}, bf16[1,512,4,128]{1,3,2,0:T(8,128)(2,1)}, u32[]{:S(2)}) copy-start(bf16[1,512,4,128]{1,3,2,0:T(8,128)(2,1)} %copy.285) | copy-start | bytes 1572868 | tf_op jit(solution)/shard_map/while
  124.1 4.2 %copy-start.2 = (bf16[1,512,4,128]{1,3,2,0:T(8,128)(2,1)S(1)}, bf16[1,512,4,128]{1,3,2,0:T(8,128)(2,1)}, u32[]{:S(2)}) copy-start(bf16[1,512,4,128]{1,3,2,0:T(8,128)(2,1)} %copy.285) | copy-start | bytes 1572868 | tf_op jit(solution)/shard_map/while
  145.5 4.2 %copy-start.2 = (bf16[1,512,4,128]{1,3,2,0:T(8,128)(2,1)S(1)}, bf16[1,512,4,128]{1,3,2,0:T(8,128)(2,1)}, u32[]{:S(2)}) copy-start(bf16[1,512,4,128]{1,3,2,0:T(8,128)(2,1)} %copy.285) | copy-start | bytes 1572868 | tf_op jit(solution)/shard_map/while
  224.2 117.1 %reduce-scatter.6.cloned.1.call-start = ((), (), s32[]{:S(2)}) async-start(), calls=%async_computation.4 | async-start | bytes 2228224 | tf_op jit(solution)/shard_map/reduce_scatter | solution.py:192
  224.7 2.2 copy-start.1
  226.9 3.6 copy-start.6
  226.9 9.5 %copy-start.4 = (bf16[64,2048]{1,0:T(8,128)(2,1)S(1)}, bf16[64,2048]{1,0:T(8,128)(2,1)}, u32[]{:S(2)}) copy-start(bf16[64,2048]{1,0:T(8,128)(2,1)} %copy-done.3) | copy-start | bytes 786436
  229.0 14.5 %copy-start.8 = (f32[64,8,64]{2,0,1:T(8,128)S(1)}, f32[64,8,64]{2,0,1:T(8,128)}, u32[]{:S(2)}) copy-start(f32[64,8,64]{2,0,1:T(8,128)} %copy-done.7) | copy-start | bytes 393220
  229.0 14.5 %copy-start.10 = (f32[64,8,64]{2,0,1:T(8,128)S(1)}, f32[64,8,64]{2,0,1:T(8,128)}, u32[]{:S(2)}) copy-start(f32[64,8,64]{2,0,1:T(8,128)} %copy-done.9) | copy-start | bytes 393220
  229.0 128.3 %reduce-scatter.8.cloned.1.call-start = ((), (), s32[]{:S(2)}) async-start(), calls=%async_computation.5 | async-start | bytes 393216 | tf_op jit(solution)/shard_map/reduce_scatter | solution.py:215
  229.1 2.1 copy-start.20
  232.1 9.6 %copy-start.17 = (f32[64,128]{1,0:T(8,128)S(1)}, f32[64,128]{1,0:T(8,128)}, u32[]{:S(2)}) copy-start(f32[64,128]{1,0:T(8,128)} %copy-done.16) | copy-start | bytes 98308
  238.5 1.6 copy-start.11
  244.9 0.6 copy-start.18
  247.1 99.4 %copy-start.12 = (bf16[64,512]{1,0:T(8,128)(2,1)S(1)}, bf16[64,512]{1,0:T(8,128)(2,1)}, u32[]{:S(2)}) copy-start(bf16[64,512]{1,0:T(8,128)(2,1)} %copy-done.11) | copy-start | bytes 196612
  247.1 99.4 %copy-start.23 = (f32[2,32]{1,0:T(2,128)S(1)}, f32[2,32]{1,0:T(2,128)}, u32[]{:S(2)}) copy-start(f32[2,32]{1,0:T(2,128)} %get-tuple-element.185) | copy-start | bytes 772
  251.4 105.9 %copy-start.13 = (bf16[64,1024]{1,0:T(8,128)(2,1)S(1)}, bf16[64,1024]{1,0:T(8,128)(2,1)}, u32[]{:S(2)}) copy-start(bf16[64,1024]{1,0:T(8,128)(2,1)} %param.18) | copy-start | bytes 393220
Sparse Core Ops, SparseCore 0:
  23.7 42.8 all-gather.1
  224.3 52.5 reduce-scatter.9
  280.7 60.5 reduce-scatter.5
  346.6 10.6 reduce-scatter.7
where the time goes:
time: 367 us; the launch traced here: 365 us
  waiting for transfers between devices  139 us (38%)
  blocking collectives  66.8 us (18%)
  matrix products  66.7 us (18%)
  local copies, waits for them, and re-layouts  47.5 us (13%)
  other arithmetic  30.8 us (8%)
  between operations  14.5 us (4%)
    reduce_scatter x1, waiting for transfers between devices, body(): lax.psum_scatter(scaled_num.astype(jnp.bfloat16), 'seq', scatter_dimensio...  63.2 us
    pmax x1, blocking collectives, body(): lax.pmax(part_max.astype(jnp.bfloat16), 'seq').astype(part_max.dtype)  59.5 us
    all_gather x1, waiting for transfers between devices, body(): query_piece = lax.all_gather(query_flat, 'seq', axis=0, tiled=True)  39.9 us
    dot_general x4, matrix products, visit(): jnp.einsum('nkgp,pkd->nkgd', weights.astype(jnp.bfloat16), values_block,...  33.2 us
    unnamed x5, waiting for transfers between devices  25.6 us
    dot_general x4, matrix products, visit(): jnp.einsum('nkgd,pkd->nkgp', grouped, keys_block, preferred_element_type=...  18.3 us
    reduce_sum x4, other arithmetic, visit(): run_sum = run_sum * factor + jnp.sum(weights, axis=-1)  16.3 us
    dynamic_slice x12, local copies, waits for them, and re-layouts, body(): lax.scan(visit, start_state, (key_blocks, value_blocks, segment_blocks))  14 us
  transfers between devices with their start and end apart: 4, of which 4 were waited for; matrix products, arithmetic and copies ran while one was open for 8% of the time, Pallas kernels for 0%

commit v1 on v0

--- a/solution.py
+++ b/solution.py
@@ -1,8 +1,11 @@
+import functools
 import math
 
 import jax
 import jax.numpy as jnp
 from jax import lax
+from jax.experimental import pallas as pl
+from jax.experimental.pallas import tpu as pltpu
 from jax.sharding import PartitionSpec as P
 
 EPSILON = 1e-06
@@ -51,6 +54,280 @@
     return jnp.einsum(
         "mdj,mjc->mdc", select, tree_rows.astype(jnp.float32), precision=lax.Precision.HIGHEST
     ).astype(jnp.bfloat16)
+
+
+def lowest(distance):
+    return distance & -distance
+
+
+def flip(index, distance):
+    out = index
+    bit = 1
+    while bit <= distance:
+        if distance & bit:
+            out = out + bit * (1 - 2 * ((index // bit) % 2))
+        bit *= 2
+    return out
+
+
+def one_bits(count):
+    bits = []
+    bit = 1
+    while bit < count:
+        bits.append(bit)
+        bit *= 2
+    return bits
+
+
+def greet(me, count):
+    barrier = pltpu.get_barrier_semaphore()
+    bits = one_bits(count)
+    for bit in bits:
+        pl.semaphore_signal(barrier, inc=1, device_id={"seq": flip(me, bit)})
+    pl.semaphore_wait(barrier, len(bits))
+
+
+def gather_kernel(count, mine_ref, all_ref, send_sem, recv_sem):
+    me = lax.axis_index("seq")
+    all_ref[me] = mine_ref[...]
+    greet(me, count)
+
+    def message(distance, owner):
+        return pltpu.make_async_remote_copy(
+            src_ref=all_ref.at[owner],
+            dst_ref=all_ref.at[owner],
+            send_sem=send_sem.at[distance],
+            recv_sem=recv_sem.at[distance],
+            device_id={"seq": flip(me, lowest(distance))},
+        )
+
+    sent = []
+    order = sorted(range(1, count), key=lambda d: (-lowest(d), d))
+    for held in [0] + order:
+        owner = flip(me, held)
+        if held:
+            message(held, owner).wait_recv()
+        top = lowest(held) if held else count
+        for bit in reversed(one_bits(top)):
+            copy = message(held | bit, owner)
+            copy.start()
+            sent.append(copy)
+    for copy in sent:
+        copy.wait_send()
+
+
+def gather_rows(mine, count):
+    return pl.pallas_call(
+        functools.partial(gather_kernel, count),
+        out_shape=jax.ShapeDtypeStruct((count,) + mine.shape, mine.dtype),
+        in_specs=[pl.BlockSpec(memory_space=pltpu.VMEM)],
+        out_specs=pl.BlockSpec(memory_space=pltpu.VMEM),
+        scratch_shapes=[pltpu.SemaphoreType.DMA((count,)), pltpu.SemaphoreType.DMA((count,))],
+        compiler_params=pltpu.CompilerParams(
+            collective_id=0, has_side_effects=True, vmem_limit_bytes=48 * 2**20
+        ),
+        name="gather_queries",
+    )(mine)
+
+
+def merge_kernel(
+    count, part_ref, lse_ref, out_ref, out_lse_ref, got, got_lse, held, held_lse, send_sem, recv_sem
+):
+    me = lax.axis_index("seq")
+    heads = part_ref.shape[2] // 128
+    greet(me, count)
+
+    def messages(distance):
+        owner = flip(me, distance)
+        if distance % 2:
+            sources = (part_ref.at[owner], lse_ref.at[owner])
+        else:
+            sources = (held.at[distance // 2], held_lse.at[distance // 2])
+        return [
+            pltpu.make_async_remote_copy(
+                src_ref=source,
+                dst_ref=target.at[distance],
+                send_sem=send_sem.at[which, distance],
+                recv_sem=recv_sem.at[which, distance],
+                device_id={"seq": flip(me, lowest(distance))},
+            )
+            for which, (source, target) in enumerate(zip(sources, (got, got_lse)))
+        ]
+
+    sent = []
+
+    def send(distance):
+        for copy in messages(distance):
+            copy.start()
+            sent.append(copy)
+
+    for distance in sorted(range(1, count, 2), reverse=True):
+        send(distance)
+    evens = sorted(range(2, count, 2), key=lambda d: (lowest(d), -d))
+    for distance in evens + [0]:
+        owner = flip(me, distance)
+        incoming = [distance | bit for bit in one_bits(lowest(distance) if distance else count)]
+        for message in incoming:
+            for copy in messages(message):
+                copy.wait_recv()
+        levels = [lse_ref[owner]] + [got_lse[message] for message in incoming]
+        top = functools.reduce(jnp.maximum, levels)
+        shares = [jnp.exp(level - top) for level in levels]
+        total = functools.reduce(jnp.add, shares)
+        inverse = 1.0 / total
+        shares = [share * inverse for share in shares]
+        new_lse = top + jnp.log(total)
+        if distance:
+            held_lse[distance // 2] = new_lse
+        else:
+            out_lse_ref[...] = new_lse
+        for head in range(heads):
+            cols = slice(head * 128, (head + 1) * 128)
+            pieces = [part_ref[owner, :, cols]] + [got[message, :, cols] for message in incoming]
+            mixed = functools.reduce(
+                jnp.add,
+                [
+                    piece.astype(jnp.float32) * share[:, head : head + 1]
+                    for piece, share in zip(pieces, shares)
+                ],
+            )
+            if distance:
+                held[distance // 2, :, cols] = mixed.astype(held.dtype)
+            else:
+                out_ref[:, cols] = mixed
+        if distance:
+            send(distance)
+    for copy in sent:
+        copy.wait_send()
+
+
+def merge_parts(parts, lse, count):
+    rows, width = parts.shape[1:]
+    lanes = lse.shape[2]
+    half = max(1, count // 2)
+    vmem = pl.BlockSpec(memory_space=pltpu.VMEM)
+    return pl.pallas_call(
+        functools.partial(merge_kernel, count),
+        out_shape=(
+            jax.ShapeDtypeStruct((rows, width), jnp.float32),
+            jax.ShapeDtypeStruct((rows, lanes), jnp.float32),
+        ),
+        in_specs=[vmem, vmem],
+        out_specs=(vmem, vmem),
+        scratch_shapes=[
+            pltpu.VMEM((count, rows, width), parts.dtype),
+            pltpu.VMEM((count, rows, lanes), jnp.float32),
+            pltpu.VMEM((half, rows, width), parts.dtype),
+            pltpu.VMEM((half, rows, lanes), jnp.float32),
+            pltpu.SemaphoreType.DMA((2, count)),
+            pltpu.SemaphoreType.DMA((2, count)),
+        ],
+        compiler_params=pltpu.CompilerParams(
+            collective_id=1, has_side_effects=True, vmem_limit_bytes=48 * 2**20
+        ),
+        name="merge_parts",
+    )(parts, lse)
+
+
+def pool_kernel(
+    groups, per_kv, block, score_scale, first_ref, last_ref, member_ref, q_ref, k_ref, v_ref, o_ref, lse_ref
+):
+    requests, tree, width = q_ref.shape
+    local_kv = k_ref.shape[1] // 128
+    per_group = requests // groups
+    o_ref[...] = jnp.zeros_like(o_ref)
+    lse_ref[...] = jnp.full(lse_ref.shape, NEGATIVE, jnp.float32)
+
+    def attend(owners, first, last):
+        count = len(owners) * per_kv * tree
+        for kv in range(local_kv):
+            keys = slice(kv * 128, (kv + 1) * 128)
+            rows = [
+                (owner, kv * per_kv + sub) for sub in range(per_kv) for owner in owners
+            ]
+            query = jnp.concatenate(
+                [q_ref[owner, :, head * 128 : (head + 1) * 128] for owner, head in rows], axis=0
+            )
+
+            def visit(step, carry):
+                run_max, run_sum, run_num = carry
+                start = pl.multiple_of(step * block, block)
+                scores = (
+                    lax.dot_general(
+                        query,
+                        k_ref[pl.ds(start, block), keys],
+                        (((1,), (1,)), ((), ())),
+                        preferred_element_type=jnp.float32,
+                    )
+                    * score_scale
+                )
+                slots = start + lax.broadcasted_iota(jnp.int32, (1, block), 1)
+                scores = jnp.where((slots >= first) & (slots < last), scores, NEGATIVE)
+                new_max = jnp.maximum(run_max, jnp.max(scores, axis=1, keepdims=True))
+                weights = jnp.exp(scores - new_max)
+                factor = jnp.exp(run_max - new_max)
+                run_sum = run_sum * factor + jnp.sum(weights, axis=1, keepdims=True)
+                run_num = run_num * factor + jnp.dot(
+                    weights.astype(jnp.bfloat16),
+                    v_ref[pl.ds(start, block), keys],
+                    preferred_element_type=jnp.float32,
+                )
+                return new_max, run_sum, run_num
+
+            run_max, run_sum, run_num = lax.fori_loop(
+                first // block,
+                (last + block - 1) // block,
+                visit,
+                (
+                    jnp.full((count, 1), NEGATIVE, jnp.float32),
+                    jnp.zeros((count, 1), jnp.float32),
+                    jnp.zeros((count, 128), jnp.float32),
+                ),
+            )
+            mixed = (run_num / run_sum).astype(o_ref.dtype)
+            lse = run_max + jnp.log(run_sum)
+            for place, (owner, head) in enumerate(rows):
+                part = slice(place * tree, (place + 1) * tree)
+                o_ref[owner, :, head * 128 : (head + 1) * 128] = mixed[part]
+                lse_ref[owner, :, head : head + 1] = lse[part]
+
+    def group_step(group, unused):
+        first, last = first_ref[group], last_ref[group]
+
+        @pl.when(last > first)
+        def _():
+            attend([member_ref[group * per_group + at] for at in range(per_group)], first, last)
+
+        return unused
+
+    def own_step(owner, unused):
+        first, last = first_ref[groups + owner], last_ref[groups + owner]
+
+        @pl.when(last > first)
+        def _():
+            attend([owner], first, last)
+
+        return unused
+
+    lax.fori_loop(0, groups, group_step, 0)
+    lax.fori_loop(0, requests, own_step, 0)
+
+
+def pool_attention(first, last, members, query, keys, values, groups, per_kv, score_scale):
+    requests, tree, width = query.shape
+    vmem = pl.BlockSpec(memory_space=pltpu.VMEM)
+    smem = pl.BlockSpec(memory_space=pltpu.SMEM)
+    return pl.pallas_call(
+        functools.partial(pool_kernel, groups, per_kv, min(512, keys.shape[0]), score_scale),
+        out_shape=(
+            jax.ShapeDtypeStruct(query.shape, jnp.bfloat16),
+            jax.ShapeDtypeStruct((requests, tree, 128), jnp.float32),
+        ),
+        in_specs=[smem, smem, smem, vmem, vmem, vmem],
+        out_specs=(vmem, vmem),
+        compiler_params=pltpu.CompilerParams(vmem_limit_bytes=48 * 2**20),
+        name="pool_attention",
+    )(first, last, members, query, keys, values)
 
 
 def body(
@@ -130,79 +407,38 @@
     tree_max = tree_max.reshape(local_tok, local_heads)
     lengths_all = jnp.concatenate([prefix_len, own_len])
     starts = jnp.cumsum(lengths_all) - lengths_all
-    slot_ids = seq_index * pool_dev + jnp.arange(pool_dev, dtype=jnp.int32)
-    slot_segment = jnp.sum((starts[None, :] <= slot_ids[:, None]).astype(jnp.int32), axis=1) - 1
-    block_len = min(512, pool_dev)
-    block_count = pool_dev // block_len
-    key_blocks = cache_keys.reshape(block_count, block_len, local_kv, head_width)
-    value_blocks = pooled_cache_values.reshape(block_count, block_len, local_kv, head_width)
-    segment_blocks = slot_segment.reshape(block_count, block_len)
-    query_flat = query.reshape(local_tok, local_heads * head_width)
-    query_piece = lax.all_gather(query_flat, "seq", axis=0, tiled=True)
-    row_ids = jnp.arange(query_piece.shape[0], dtype=jnp.int32)
-    owners = row_ids // tree
-    count = query_piece.shape[0]
-    grouped = query_piece.reshape(count, local_kv, per_kv, head_width)
-    owner_pick = (owners[:, None] == all_reqs[None, :]).astype(jnp.int32)
-    known = owners >= 0
-    prefix_segment = jnp.where(known, jnp.sum(owner_pick * request_group[None, :], axis=1), -5)
-    own_segment = jnp.where(known, owners + groups, -5)
-
-    def visit(carry, block):
-        run_max, run_sum, run_num = carry
-        keys_block, values_block, segment_block = block
-        scores = (
-            jnp.einsum("nkgd,pkd->nkgp", grouped, keys_block, preferred_element_type=jnp.float32)
-            * score_scale
-        )
-        visible = (segment_block[None, :] == prefix_segment[:, None]) | (
-            segment_block[None, :] == own_segment[:, None]
-        )
-        visible = visible[:, None, None, :]
-        scores = jnp.where(visible, scores, NEGATIVE)
-        new_max = jnp.maximum(run_max, jnp.max(scores, axis=-1))
-        weights = jnp.where(visible, jnp.exp(scores - new_max[..., None]), 0.0)
-        factor = jnp.exp(run_max - new_max)
-        run_sum = run_sum * factor + jnp.sum(weights, axis=-1)
-        run_num = run_num * factor[..., None] + jnp.einsum(
-            "nkgp,pkd->nkgd",
-            weights.astype(jnp.bfloat16),
-            values_block,
-            preferred_element_type=jnp.float32,
-        )
-        return ((new_max, run_sum, run_num), None)
-
-    start_state = (
-        jnp.full((count, local_kv, per_kv), NEGATIVE, jnp.float32),
-        jnp.zeros((count, local_kv, per_kv), jnp.float32),
-        jnp.zeros((count, local_kv, per_kv, head_width), jnp.float32),
-    )
-    final_state, unused = lax.scan(visit, start_state, (key_blocks, value_blocks, segment_blocks))
-    run_max, run_sum, run_num = final_state
-    part_max = run_max.reshape(count, local_heads)
-    part_sum = run_sum.reshape(count, local_heads)
-    part_num = run_num.reshape(count, local_heads * head_width)
-    all_rows = part_max.shape[0]
-    cache_max = lax.pmax(part_max.astype(jnp.bfloat16), "seq").astype(part_max.dtype)
-    factor = jnp.exp(part_max - cache_max)
-    scaled_num = (part_num.reshape(all_rows, local_heads, head_width) * factor[..., None]).reshape(
-        all_rows, local_heads * head_width
-    )
-    summed_num, summed_sum = (
-        lax.psum_scatter(
-            scaled_num.astype(jnp.bfloat16), "seq", scatter_dimension=0, tiled=True
-        ).astype(jnp.float32),
-        lax.psum_scatter(
-            (part_sum * factor).astype(jnp.bfloat16), "seq", scatter_dimension=0, tiled=True
-        ).astype(jnp.float32),
-    )
-    own_max = lax.dynamic_slice_in_dim(cache_max, seq_index * local_tok, local_tok, 0)
-    final_max = jnp.maximum(own_max, tree_max)
-    cache_factor = jnp.exp(own_max - final_max)
+    seq_count = requests // local_req
+    first = jnp.clip(starts - seq_index * pool_dev, 0, pool_dev)
+    last = jnp.clip(starts + lengths_all - seq_index * pool_dev, 0, pool_dev)
+    same = (request_group[:, None] == request_group[None, :]) & (all_reqs[None, :] < all_reqs[:, None])
+    place = request_group * (requests // groups) + jnp.sum(same.astype(jnp.int32), axis=1)
+    members = jnp.sum(
+        (place[None, :] == all_reqs[:, None]).astype(jnp.int32) * all_reqs[None, :], axis=1
+    )
+    gathered = gather_rows(query.reshape(local_tok, local_heads * head_width), seq_count)
+    parts, part_lse = pool_attention(
+        first,
+        last,
+        members,
+        gathered.reshape(requests, tree, local_heads * head_width),
+        cache_keys.reshape(pool_dev, local_kv * head_width),
+        pooled_cache_values.reshape(pool_dev, local_kv * head_width),
+        groups,
+        per_kv,
+        score_scale,
+    )
+    cache_mix, cache_lse = merge_parts(
+        parts.reshape(seq_count, local_tok, local_heads * head_width),
+        part_lse.reshape(seq_count, local_tok, 128),
+        seq_count,
+    )
+    cache_lse = cache_lse[:, :local_heads]
+    final_max = jnp.maximum(cache_lse, tree_max)
+    cache_factor = jnp.exp(cache_lse - final_max)
     tree_factor = jnp.exp(tree_max - final_max)
-    weight_sum = summed_sum * cache_factor + tree_sum * tree_factor
+    weight_sum = cache_factor + tree_sum * tree_factor
     mixed = (
-        summed_num.reshape(local_tok, local_heads, head_width) * cache_factor[..., None]
+        cache_mix.reshape(local_tok, local_heads, head_width) * cache_factor[..., None]
         + tree_num * tree_factor[..., None]
     )
     mixed = mixed / weight_sum[..., None]

time: 367 us -> 138 us (0.38)
  waiting for transfers between devices: 139 us -> 10.8 us
  Pallas kernels: 0 us -> 62.6 us
  blocking collectives: 66.8 us -> 7.5 us
  matrix products: 66.7 us -> 12.1 us
  local copies, waits for them, and re-layouts: 47.5 us -> 18.4 us
  other arithmetic: 30.8 us -> 9.86 us
    reduce_scatter x1 -> x0, waiting for transfers between devices: 63.2 us -> none  [body(): lax.psum_scatter(scaled_num.astype(jnp.bfloat16), 'seq', scatter_dimensio...]
    pallas_call x0 -> x3, Pallas kernels: none -> 62.6 us  [the longest x1 26.4 us: merge_parts(): pl.pallas_call(functools.partial(merge_kernel, count), out_shape=(jax.Sha...]
    pmax x1 -> x0, blocking collectives: 59.5 us -> none  [body(): lax.pmax(part_max.astype(jnp.bfloat16), 'seq').astype(part_max.dtype)]
    dot_general x8 -> x0, matrix products: 51.5 us -> none  [the longest x4 33.2 us: visit(): jnp.einsum('nkgp,pkd->nkgd', weights.astype(jnp.bfloat16), values_block,...]
    all_gather x1 -> x0, waiting for transfers between devices: 39.9 us -> none  [body(): query_piece = lax.all_gather(query_flat, 'seq', axis=0, tiled=True)]
    unnamed x5 -> x1, waiting for transfers between devices: 25.6 us -> 0.02 us
    reduce_sum x6 -> x2, other arithmetic: 16.5 us -> 0.29 us  [the longest x1 0.18 us: body(): jnp.sum(same.astype(jnp.int32), axis=1)]
    dynamic_slice x12 -> x0, local copies, waits for them, and re-layouts: 14 us -> none  [body(): lax.scan(visit, start_state, (key_blocks, value_blocks, segment_blocks))]
  transfers between devices with their start and end apart: 4 -> 1, of which waited for: 4 -> 1; matrix products, arithmetic and copies ran while one was open for 8% -> 1% of each run, Pallas kernels for 0% -> 0%
where the time goes in v1:
time: 138 us; the launch traced here: 136 us
  Pallas kernels  62.6 us (45%)
  local copies, waits for them, and re-layouts  18.4 us (13%)
  between operations  14.7 us (11%)
  matrix products  12.1 us (9%)
  waiting for transfers between devices  10.8 us (8%)
  other arithmetic  9.86 us (7%)
  blocking collectives  7.5 us (5%)
    pallas_call x1, Pallas kernels, merge_parts(): pl.pallas_call(functools.partial(merge_kernel, count), out_shape=(jax.Sha...  26.4 us
    pallas_call x1, Pallas kernels, gather_rows(): pl.pallas_call(functools.partial(gather_kernel, count), out_shape=jax.Sha...  20.9 us
    pallas_call x1, Pallas kernels, pool_attention(): pl.pallas_call(functools.partial(pool_kernel, groups, per_kv, min(512, ke...  15.3 us
    reduce_scatter x1, waiting for transfers between devices, body(): lax.psum_scatter(projected.astype(jnp.bfloat16), 'kv', scatter_dimension=...  10.8 us
    all_gather x1, blocking collectives, body(): full_rows = lax.all_gather(hidden, 'kv', axis=1, tiled=True)  7.5 us
    dot_general x1, matrix products, body(): jnp.dot(normed, w_query, preferred_element_type=jnp.float32)  3.12 us
  transfers between devices with their start and end apart: 1, of which 1 were waited for; matrix products, arithmetic and copies ran while one was open for 1% of the time, Pallas kernels for 0%

profile of v1, /device:TPU:0, one launch (start us, length us, event | category | flops | bytes accessed | tf_op | source)
XLA Modules:
  0.0 136.0 jit_solution(13352784424291471987)
XLA Ops:
  7.3 7.5 %all_gather.3 = bf16[64,2048]{1,0:T(8,128)(2,1)S(1)} all-gather(bf16[64,1024]{1,0:T(8,128)(2,1)} %param.16), channel_id=1, replica_groups=mesh['kv'=2,'seq'=16] {'kv'}, dimensions={1}, use_global_device_ids=true | all-gather | bytes 393216 | tf_op jit(solution)/shard_map/all_gather | solution.py:362
  14.8 0.2 fusion.5
  14.9 1.2 fusion.67
  16.2 0.7 reshape.258
  17.0 3.1 %fusion.69 = f32[64,1024]{1,0:T(8,128)S(1)} fusion(bf16[2048,1024]{1,0:T(8,128)(2,1)} %param.18, bf16[64,2048]{1,0:T(8,128)(2,1)S(1)} %all_gather.3, f32[2048]{0:T(1024)S(1)} %copy-done.14, f32[64]{0:T(128)S(1)} %add_rsqrt_fusion.2), kind=kOutput, calls=%fused_computation.139 | convolution fusion | flops 268959744 | bytes 4727040 | tf_op jit(solution)/shard_map/dot_general | solution.py:375
  20.2 0.1 multiply_reduce_fusion
  20.4 0.7 rsqrt.36
  21.1 0.7 copy.141
  21.8 0.6 broadcast_bitcast_fusion
  22.3 0.1 fusion.13
  22.5 0.9 reshape.260
  23.4 0.2 convert_reduce_fusion
  23.6 0.1 select_reduce_fusion.member_ref
  23.8 0.2 select_reduce_fusion.1
  24.0 0.2 fusion.58
  24.2 0.2 convolution_minimum_fusion.4
  24.4 0.2 convolution_minimum_fusion.3
  24.6 0.2 convolution_minimum_fusion.2
  24.8 0.2 convolution_minimum_fusion.1
  24.9 0.2 fusion.74
  25.3 0.6 broadcast_add_fusion
  26.0 0.1 copy.104
  26.1 0.7 reduce
  26.8 0.8 multiply_cosine_fusion
  27.6 0.2 multiply_sine_fusion.1
  27.8 0.7 pad_maximum_fusion.1
  28.5 0.7 pad_maximum_fusion
  29.2 0.2 fusion.4
  29.5 0.7 copy.126
  30.2 2.1 %convolution_convert_fusion.2 = bf16[64,512]{1,0:T(8,128)(2,1)S(1)} fusion(bf16[2048,512]{1,0:T(8,128)(2,1)} %param.20, bf16[64,2048]{1,0:T(8,128)(2,1)S(1)} %all_gather.3, f32[2048]{0:T(1024)S(1)} %copy-done.14, f32[64]{0:T(128)S(1)} %add_rsqrt_fusion.2), kind=kOutput, calls=%fused_computation.8 | convolution fusion | flops 134774784 | bytes 2433280 | tf_op jit(solution)/shard_map/dot_general | solution.py:384
  32.3 0.6 reshape_reshape.6
  33.0 0.1 multiply_reduce_fusion.1
  33.2 0.7 rsqrt.35
  34.0 0.1 slice_negate_fusion.1
  34.1 0.1 slice_negate_fusion
  34.3 0.9 pad_maximum_fusion.2
  35.2 1.4 %fusion.75 = (f32[2,32,4,2]{1,3,2,0:T(2,128)S(1)}, f32[2,32,4,2,32]{1,4,3,2,0:T(8,128)S(1)}) fusion(pred[2,32,32]{1,2,0:T(8,128)(4,1)S(1)} %copy.111, f32[2,32,4,2,64]{4,1,0,3,2:T(8,128)S(1)} %bitcast.125, f32[2,32,4,2,64]{4,1,0,3,2:T(8,128)S(1)} %bitcast.124, f32[2,32,4,2,128]{4,3,2,1,0:T(2,128)} %reshape.260, f32[2,32,128]{2,1,0:T(8,128)S(1)} %get-tuple-element.35, ...), kind=kOutput, calls=%fused_computation.142 | convolution fusion | flops 4931072 | bytes 925696 | tf_op jit(solution)/shard_map/atkgd,askd->atkgs/dot_general | solution.py:393
  36.6 0.6 copy.118
  37.2 0.7 fusion.19
  37.9 0.9 convolution_bitcast_fusion
  38.8 1.4 %reshape.261 = f32[64,8]{0,1:T(8,128)} reshape(f32[2,32,4,2]{1,0,3,2:T(2,128)} %copy.118) | data formatting | bytes 4096 | tf_op jit(solution)/shard_map/reshape | solution.py:407
  40.2 1.2 copy.122
  41.3 0.9 reshape.262
  42.3 0.7 copy.124
  43.1 0.8 copy.119
  43.9 0.9 mul.345
  44.9 1.2 mul.325.clone
  46.1 1.0 fusion.11.mine_ref
  47.1 20.9 %gather_queries.1 = bf16[16,64,1024]{2,1,0:T(8,128)(2,1)S(1)} custom-call(bf16[64,1024]{1,0:T(8,128)(2,1)S(1)} %fusion.11.mine_ref), custom_call_target="tpu_custom_call" | custom-call | tf_op jit(solution)/shard_map/gather_queries/pallas_call | solution.py:120
  68.1 2.6 %copy_bitcast_fusion = (bf16[2048,512]{1,0:T(8,128)(2,1)}, bf16[2048,512]{1,0:T(8,128)(2,1)}) fusion(bf16[256,8,4,128]{3,2,1,0:T(4,128)(2,1)S(1)} %bitcast.126, bf16[256,8,4,128]{3,2,1,0:T(4,128)(2,1)S(1)} %bitcast.127), kind=kLoop, calls=%fused_computation.1 | loop fusion | bytes 8388608 | tf_op jit(solution)/shard_map/reshape | solution.py:425
  70.7 15.3 %pool_attention.1 = (bf16[32,32,1024]{2,1,0:T(8,128)(2,1)S(1)}, f32[32,32,128]{2,1,0:T(8,128)S(1)}) custom-call(s32[36]{0:T(128)S(1)} %get-tuple-element.29.first_ref, s32[36]{0:T(128)S(1)} %get-tuple-element.28.last_ref, s32[32]{0:T(128)S(1)} %select_reduce_fusion.member_ref, bf16[32,32,1024]{2,1,0:T(8,128)(2,1)S(1)} %bitcast.119, ...), custom_call_target="tpu_custom_call" | custom-call | tf_op jit(solution)/shard_map/pool_attention/pallas_call | solution.py:320
  86.0 26.4 %merge_parts.1 = (f32[64,1024]{1,0:T(8,128)S(1)}, f32[64,128]{1,0:T(8,128)S(1)}) custom-call(bf16[16,64,1024]{2,1,0:T(8,128)(2,1)S(1)} %bitcast.120, f32[16,64,128]{2,1,0:T(8,128)S(1)} %bitcast.121), custom_call_target="tpu_custom_call" | custom-call | tf_op jit(solution)/shard_map/merge_parts/pallas_call | solution.py:209
  112.5 0.1 mul.388
  112.6 0.1 div.38
  112.8 0.1 mul.384
  112.9 0.1 mul.381
  113.1 1.6 %convolution_convert_fusion = bf16[64,2048]{1,0:T(8,128)(2,1)} fusion(bf16[1024,2048]{1,0:T(8,128)(2,1)S(1)} %copy-done.1, f32[8,8,8,128]{3,2,1,0:T(8,128)S(1)} %bitcast.130, f32[8,8,8,128]{3,2,1,0:T(8,128)S(1)} %bitcast.131, f32[64,1024]{1,0:T(8,128)S(1)} %copy-done.4, f32[8,8,8,128]{3,2,1,0:T(8,128)S(1)} %bitcast.132, f32[64,1024]{1,0:T(8,128)S(1)} %get-tuple-element.9, ...), kind=kOutput, calls=%fused_computation | convolution fusion | flops 268959744 | bytes 6029312 | tf_op jit(solution)/shard_map/dot_general | solution.py:450
  114.9 0.1 maximum_multiply_fusion.3
  115.1 0.1 fusion.56
  115.3 0.1 mul.364.clone
  115.7 0.3 convolution_convert_fusion.1
  116.1 0.7 fusion.73
  116.7 10.8 %reduce-scatter.2.cloned.1.call-done = bf16[64,1024]{1,0:T(8,128)(2,1)} async-done(((bf16[64,2048]{1,0:T(8,128)(2,1)}), bf16[64,1024]{1,0:T(8,128)(2,1)}) %reduce-scatter.2.cloned.1.call-update) | async-done | bytes 131088 | tf_op jit(solution)/shard_map/reduce_scatter | solution.py:451
  127.5 1.6 %add_convert_fusion = bf16[64,1024]{1,0:T(8,128)(2,1)} fusion(bf16[64,1024]{1,0:T(8,128)(2,1)S(1)} %copy-done.7, bf16[64,1024]{1,0:T(8,128)(2,1)} %reduce-scatter.2.cloned.1.call-done), kind=kLoop, calls=%fused_computation.45 | loop fusion | flops 262144 | bytes 393216 | tf_op jit(solution)/shard_map/convert_element_type | solution.py:454
  (91 shorter events, 1.7 us)
Async XLA Ops:
  7.2 7.8 %copy-start = (bf16[2048,512]{1,0:T(8,128)(2,1)S(1)}, bf16[2048,512]{1,0:T(8,128)(2,1)}, u32[]{:S(2)}) copy-start(bf16[2048,512]{1,0:T(8,128)(2,1)} %param.19) | copy-start | bytes 6291460
  7.2 9.8 %copy-start.14 = (f32[2048]{0:T(1024)S(1)}, f32[2048]{0:T(1024)}, u32[]{:S(2)}) copy-start(f32[2048]{0:T(1024)} %param.17) | copy-start | bytes 24580
  7.2 120.3 %reduce-scatter.2.cloned.1.call-start = ((), (), s32[]{:S(2)}) async-start(), calls=%async_computation.1 | async-start | bytes 393216 | tf_op jit(solution)/shard_map/reduce_scatter | solution.py:451
  16.9 4.8 %copy-start.15 = (f32[128]{0:T(128)S(1)}, f32[128]{0:T(128)}, u32[]{:S(2)}) copy-start(f32[128]{0:T(128)} %param.23) | copy-start | bytes 1540
  16.9 6.5 %copy-start.23 = (s32[32]{0:T(128)S(1)}, s32[32]{0:T(128)}, u32[]{:S(2)}) copy-start(s32[32]{0:T(128)} %param.29) | copy-start | bytes 388
  16.9 6.8 %copy-start.19 = (s32[32]{0:T(128)S(1)}, s32[32]{0:T(128)}, u32[]{:S(2)}) copy-start(s32[32]{0:T(128)} %param.28) | copy-start | bytes 388
  16.9 6.8 %copy-start.24 = (s32[4]{0:T(128)S(1)}, s32[4]{0:T(128)}, u32[]{:S(2)}) copy-start(s32[4]{0:T(128)} %param.27) | copy-start | bytes 52
  17.0 7.2 %copy-start.22 = (s32[2,32]{1,0:T(2,128)S(1)}, s32[2,32]{1,0:T(2,128)}, u32[]{:S(2)}) copy-start(s32[2,32]{1,0:T(2,128)} %param.30) | copy-start | bytes 772
  20.1 9.1 %copy-start.26 = (bf16[2048,8]{0,1:T(8,128)(2,1)S(1)}, bf16[2048,8]{0,1:T(8,128)(2,1)}, u32[]{:S(2)}) copy-start(bf16[2048,8]{0,1:T(8,128)(2,1)} %param.21) | copy-start | bytes 98308
  24.2 9.7 %copy-start.16 = (f32[128]{0:T(128)S(1)}, f32[128]{0:T(128)}, u32[]{:S(2)}) copy-start(f32[128]{0:T(128)} %param.24) | copy-start | bytes 1540
  25.2 4.3 %copy-start.9 = (f32[2,32,32]{2,1,0:T(8,128)}, f32[2,32,32]{2,1,0:T(8,128)S(1)}, u32[]{:S(2)}) copy-start(f32[2,32,32]{2,1,0:T(8,128)S(1)} %get-tuple-element.31) | copy-start | bytes 24580
  32.3 1.7 %copy-start.5 = (bf16[64,512]{1,0:T(8,128)(2,1)}, bf16[64,512]{1,0:T(8,128)(2,1)S(1)}, u32[]{:S(2)}) copy-start(bf16[64,512]{1,0:T(8,128)(2,1)S(1)} %convolution_convert_fusion.2) | copy-start | bytes 196612
  33.9 4.0 %copy-start.12 = (bf16[2,32,4,128]{3,2,1,0:T(4,128)(2,1)S(1)}, bf16[2,32,4,128]{3,2,1,0:T(4,128)(2,1)}, u32[]{:S(2)}) copy-start(bf16[2,32,4,128]{3,2,1,0:T(4,128)(2,1)} %reshape_reshape.6) | copy-start | bytes 196612
  43.9 24.1 %copy-start.20 = (s32[32]{0:T(128)S(1)}, s32[32]{0:T(128)}, u32[]{:S(2)}) copy-start(s32[32]{0:T(128)} %param.28) | copy-start | bytes 388
  43.9 24.1 %copy-start.21 = (s32[36]{0:T(128)S(1)}, s32[36]{0:T(128)}, u32[]{:S(2)}) copy-start(s32[36]{0:T(128)} %reduce) | copy-start | bytes 436
  43.9 24.1 %copy-start.25 = (s32[4]{0:T(128)S(1)}, s32[4]{0:T(128)}, u32[]{:S(2)}) copy-start(s32[4]{0:T(128)} %param.27) | copy-start | bytes 52
  43.9 24.2 %copy-start.2 = (bf16[2048,4,128]{2,1,0:T(4,128)(2,1)S(1)}, bf16[2048,4,128]{2,1,0:T(4,128)(2,1)}, u32[]{:S(2)}) copy-start(bf16[2048,4,128]{2,1,0:T(4,128)(2,1)} %param.26) | copy-start | bytes 6291460
  43.9 24.1 %copy-start.3 = (bf16[2048,4,128]{2,1,0:T(4,128)(2,1)S(1)}, bf16[2048,4,128]{2,1,0:T(4,128)(2,1)}, u32[]{:S(2)}) copy-start(bf16[2048,4,128]{2,1,0:T(4,128)(2,1)} %param.25) | copy-start | bytes 6291460
  70.7 42.3 %copy-start.1 = (bf16[1024,2048]{1,0:T(8,128)(2,1)S(1)}, bf16[1024,2048]{1,0:T(8,128)(2,1)}, u32[]{:S(2)}) copy-start(bf16[1024,2048]{1,0:T(8,128)(2,1)} %param.22) | copy-start | bytes 12582916
  86.0 26.5 %copy-start.13 = (f32[64,8]{1,0:T(8,128)S(1)}, f32[64,8]{1,0:T(8,128)}, u32[]{:S(2)}) copy-start(f32[64,8]{1,0:T(8,128)} %copy.126) | copy-start | bytes 6148
  86.0 27.0 %copy-start.4 = (f32[64,1024]{1,0:T(8,128)S(1)}, f32[64,1024]{1,0:T(8,128)}, u32[]{:S(2)}) copy-start(f32[64,1024]{1,0:T(8,128)} %reshape.262) | copy-start | bytes 786436
  113.1 1.7 %copy-start.17 = (f32[128]{0:T(128)S(1)}, f32[128]{0:T(128)}, u32[]{:S(2)}) copy-start(f32[128]{0:T(128)} %param.24) | copy-start | bytes 1540
  113.1 1.8 %copy-start.11 = (f32[64,128]{1,0:T(8,128)S(1)}, f32[64,128]{1,0:T(8,128)}, u32[]{:S(2)}) copy-start(f32[64,128]{1,0:T(8,128)} %pad_maximum_fusion.1) | copy-start | bytes 98308
  113.1 1.9 %copy-start.27 = (s32[2]{0:T(128)S(1)}, s32[2]{0:T(128)}, u32[]{:S(2)}) copy-start(s32[2]{0:T(128)} %param.31) | copy-start | bytes 28
  113.1 2.0 %copy-start.10 = (f32[2,32,32]{2,1,0:T(8,128)S(1)}, f32[2,32,32]{2,1,0:T(8,128)}, u32[]{:S(2)}) copy-start(f32[2,32,32]{2,1,0:T(8,128)} %copy-done.9) | copy-start | bytes 24580
  113.1 2.1 %copy-start.8 = (f32[64,128]{1,0:T(8,128)S(1)}, f32[64,128]{1,0:T(8,128)}, u32[]{:S(2)}) copy-start(f32[64,128]{1,0:T(8,128)} %pad_maximum_fusion) | copy-start | bytes 98308
  114.7 1.0 copy-start.6
  114.7 1.0 copy-start.18
  114.7 12.8 %copy-start.7 = (bf16[64,1024]{1,0:T(8,128)(2,1)S(1)}, bf16[64,1024]{1,0:T(8,128)(2,1)}, u32[]{:S(2)}) copy-start(bf16[64,1024]{1,0:T(8,128)(2,1)} %param.16) | copy-start | bytes 393220
Sparse Core Ops, SparseCore 0:
  114.9 12.5 reduce-scatter.1

commit v2 on v1

--- a/solution.py
+++ b/solution.py
@@ -18,16 +18,18 @@
     return values * lax.rsqrt(mean_square + EPSILON) * scales
 
 
-def rotate_pairs(values, positions):
-    half_width = values.shape[-1] // 2
+def rope_tables(positions, head_width):
+    half_width = head_width // 2
     freqs = jnp.exp(
-        jnp.arange(half_width, dtype=jnp.float32) * (-2.0 * math.log(ROPE_BASE) / values.shape[-1])
+        jnp.arange(half_width, dtype=jnp.float32) * (-2.0 * math.log(ROPE_BASE) / head_width)
     )
     angles = positions[:, None] * freqs[None, :]
-    cosine = jnp.concatenate([jnp.cos(angles), jnp.cos(angles)], axis=-1)[:, None, :]
-    sine = jnp.concatenate([jnp.sin(angles), jnp.sin(angles)], axis=-1)[:, None, :]
-    turned = jnp.concatenate([-values[..., half_width:], values[..., :half_width]], axis=-1)
-    return values * cosine + turned * sine
+    cosine = jnp.cos(angles)
+    sine = jnp.sin(angles)
+    return (
+        jnp.concatenate([cosine, cosine], axis=-1),
+        jnp.concatenate([-sine, sine], axis=-1),
+    )
 
 
 def tree_paths(parents):
@@ -79,18 +81,87 @@
     return bits
 
 
-def greet(me, count):
+def greet(me, count, kv, kv_count):
     barrier = pltpu.get_barrier_semaphore()
     bits = one_bits(count)
     for bit in bits:
         pl.semaphore_signal(barrier, inc=1, device_id={"seq": flip(me, bit)})
-    pl.semaphore_wait(barrier, len(bits))
-
-
-def gather_kernel(count, mine_ref, all_ref, send_sem, recv_sem):
+    for hop in range(1, kv_count):
+        pl.semaphore_signal(barrier, inc=1, device_id={"kv": (kv + hop) % kv_count})
+    pl.semaphore_wait(barrier, len(bits) + kv_count - 1)
+
+
+def layer_kernel(
+    count,
+    kv_count,
+    score_scale,
+    hidden_ref,
+    in_gain_ref,
+    w_query_ref,
+    w_key_ref,
+    w_value_ref,
+    w_gate_ref,
+    q_gain_ref,
+    k_gain_ref,
+    cos_ref,
+    sin_ref,
+    seen_ref,
+    all_ref,
+    key_ref,
+    value_ref,
+    tree_ref,
+    tree_lse_ref,
+    gate_ref,
+    wide,
+    w_query,
+    w_key,
+    w_value,
+    load_sem,
+    wide_send,
+    wide_recv,
+    send_sem,
+    recv_sem,
+):
     me = lax.axis_index("seq")
-    all_ref[me] = mine_ref[...]
-    greet(me, count)
+    kv = lax.axis_index("kv")
+    loads = [
+        pltpu.make_async_copy(source, target, load_sem.at[which])
+        for which, (source, target) in enumerate(
+            [(w_query_ref, w_query), (w_key_ref, w_key), (w_value_ref, w_value)]
+        )
+    ]
+    for load in loads:
+        load.start()
+    wide[kv] = hidden_ref[...]
+    greet(me, count, kv, kv_count)
+
+    def wide_message(hop, owner):
+        return pltpu.make_async_remote_copy(
+            src_ref=wide.at[owner],
+            dst_ref=wide.at[owner],
+            send_sem=wide_send.at[hop],
+            recv_sem=wide_recv.at[hop],
+            device_id={"kv": (kv + hop) % kv_count},
+        )
+
+    wide_sent = [wide_message(hop, kv) for hop in range(1, kv_count)]
+    for copy in wide_sent:
+        copy.start()
+    for hop in range(1, kv_count):
+        wide_message(hop, (kv + kv_count - hop) % kv_count).wait_recv()
+    rows = jnp.concatenate([wide[at] for at in range(kv_count)], axis=1).astype(jnp.float32)
+    normed = rms_scale(rows, in_gain_ref[...]).astype(jnp.bfloat16)
+
+    def rotated(values, gain_ref):
+        values = rms_scale(values, gain_ref[...])
+        return (values * cos_ref[...] + pltpu.roll(values, 64, 1) * sin_ref[...]).astype(jnp.bfloat16)
+
+    loads[0].wait()
+    query = jnp.dot(normed, w_query[...], preferred_element_type=jnp.float32)
+    heads = query.shape[1] // 128
+    queries = [rotated(query[:, h * 128 : (h + 1) * 128], q_gain_ref) for h in range(heads)]
+    for head in range(heads):
+        all_ref[me, :, head * 128 : (head + 1) * 128] = queries[head]
 
     def message(distance, owner):
         return pltpu.make_async_remote_copy(
@@ -102,40 +173,150 @@
         )
 
     sent = []
-    order = sorted(range(1, count), key=lambda d: (-lowest(d), d))
-    for held in [0] + order:
-        owner = flip(me, held)
-        if held:
-            message(held, owner).wait_recv()
-        top = lowest(held) if held else count
-        for bit in reversed(one_bits(top)):
-            copy = message(held | bit, owner)
+
+    def hand_on(distance):
+        owner = flip(me, distance)
+        if distance:
+            message(distance, owner).wait_recv()
+        for bit in reversed(one_bits(lowest(distance) if distance else count)):
+            copy = message(distance | bit, owner)
             copy.start()
             sent.append(copy)
-    for copy in sent:
+
+    hand_on(0)
+    local_kv = key_ref.shape[1] // 128
+    per_kv = heads // local_kv
+    tokens = hidden_ref.shape[0]
+
+    def keys_work():
+        loads[1].wait()
+        key = jnp.dot(normed, w_key[...], preferred_element_type=jnp.float32)
+        for at in range(local_kv):
+            cols = slice(at * 128, (at + 1) * 128)
+            key_ref[:, cols] = rotated(key[:, cols], k_gain_ref)
+
+    def values_work():
+        loads[2].wait()
+        value_ref[...] = jnp.dot(
+            normed, w_value[...], preferred_element_type=jnp.float32
+        ).astype(jnp.bfloat16)
+        gate_ref[...] = jax.nn.sigmoid(
+            jnp.dot(normed, w_gate_ref[...], preferred_element_type=jnp.float32)
+        )
+        tree_lse_ref[...] = jnp.zeros(tree_lse_ref.shape, jnp.float32)
+
+    def tree_work(at):
+        cols = slice(at * 128, (at + 1) * 128)
+        stacked = jnp.concatenate(queries[at * per_kv : (at + 1) * per_kv], axis=0)
+        scores = (
+            lax.dot_general(
+                stacked,
+                key_ref[:, cols],
+                (((1,), (1,)), ((), ())),
+                preferred_element_type=jnp.float32,
+            )
+            * score_scale
+        )
+        seen = jnp.concatenate([seen_ref[...]] * per_kv, axis=0) > 0.5
+        scores = jnp.where(seen, scores, NEGATIVE)
+        top = jnp.max(scores, axis=1, keepdims=True)
+        weights = jnp.where(seen, jnp.exp(scores - top), 0.0)
+        total = jnp.sum(weights, axis=1, keepdims=True)
+        mixed = (
+            jnp.dot(
+                weights.astype(jnp.bfloat16), value_ref[:, cols], preferred_element_type=jnp.float32
+            )
+            / total
+        )
+        lse = top + jnp.log(total)
+        for sub in range(per_kv):
+            head = at * per_kv + sub
+            part = slice(sub * tokens, (sub + 1) * tokens)
+            tree_ref[:, head * 128 : (head + 1) * 128] = mixed[part]
+            tree_lse_ref[:, head : head + 1] = lse[part]
+
+    work = [keys_work, values_work] + [functools.partial(tree_work, at) for at in range(local_kv)]
+    order = sorted(range(2, count, 2), key=lambda d: (-lowest(d), d))
+    for distance in order:
+        if work:
+            work.pop(0)()
+        hand_on(distance)
+    for rest in work:
+        rest()
+    for distance in range(1, count, 2):
+        hand_on(distance)
+    for copy in wide_sent + sent:
         copy.wait_send()
 
 
-def gather_rows(mine, count):
+def layer_front(
+    hidden, in_gain, w_query, w_key, w_value, w_gate, q_gain, k_gain, cosine, sine, seen, count, kv_count, score_scale
+):
+    tokens = hidden.shape[0]
+    width = w_query.shape[1]
+    vmem = pl.BlockSpec(memory_space=pltpu.VMEM)
+    anywhere = pl.BlockSpec(memory_space=pl.ANY)
     return pl.pallas_call(
-        functools.partial(gather_kernel, count),
-        out_shape=jax.ShapeDtypeStruct((count,) + mine.shape, mine.dtype),
-        in_specs=[pl.BlockSpec(memory_space=pltpu.VMEM)],
-        out_specs=pl.BlockSpec(memory_space=pltpu.VMEM),
-        scratch_shapes=[pltpu.SemaphoreType.DMA((count,)), pltpu.SemaphoreType.DMA((count,))],
+        functools.partial(layer_kernel, count, kv_count, score_scale),
+        out_shape=(
+            jax.ShapeDtypeStruct((count, tokens, width), jnp.bfloat16),
+            jax.ShapeDtypeStruct((tokens, w_key.shape[1]), jnp.bfloat16),
+            jax.ShapeDtypeStruct((tokens, w_value.shape[1]), jnp.bfloat16),
+            jax.ShapeDtypeStruct((tokens, width), jnp.float32),
+            jax.ShapeDtypeStruct((tokens, 128), jnp.float32),
+            jax.ShapeDtypeStruct((tokens, w_gate.shape[1]), jnp.float32),
+        ),
+        in_specs=[vmem, vmem, anywhere, anywhere, anywhere] + [vmem] * 6,
+        out_specs=(vmem,) * 6,
+        scratch_shapes=[
+            pltpu.VMEM((kv_count,) + hidden.shape, hidden.dtype),
+            pltpu.VMEM(w_query.shape, w_query.dtype),
+            pltpu.VMEM(w_key.shape, w_key.dtype),
+            pltpu.VMEM(w_value.shape, w_value.dtype),
+            pltpu.SemaphoreType.DMA((3,)),
+            pltpu.SemaphoreType.DMA((kv_count,)),
+            pltpu.SemaphoreType.DMA((kv_count,)),
+            pltpu.SemaphoreType.DMA((count,)),
+            pltpu.SemaphoreType.DMA((count,)),
+        ],
         compiler_params=pltpu.CompilerParams(
             collective_id=0, has_side_effects=True, vmem_limit_bytes=48 * 2**20
         ),
-        name="gather_queries",
-    )(mine)
+        name="layer_front",
+    )(hidden, in_gain[None], w_query, w_key, w_value, w_gate, q_gain[None], k_gain[None], cosine, sine, seen)
 
 
 def merge_kernel(
-    count, part_ref, lse_ref, out_ref, out_lse_ref, got, got_lse, held, held_lse, send_sem, recv_sem
+    count,
+    kv_count,
+    part_ref,
+    lse_ref,
+    tree_ref,
+    tree_lse_ref,
+    gate_ref,
+    w_out_ref,
+    hidden_ref,
+    out_ref,
+    got,
+    got_lse,
+    held,
+    held_lse,
+    w_out,
+    attended,
+    outgoing,
+    arrived,
+    send_sem,
+    recv_sem,
+    load_sem,
+    out_send,
+    out_recv,
 ):
     me = lax.axis_index("seq")
+    kv = lax.axis_index("kv")
     heads = part_ref.shape[2] // 128
-    greet(me, count)
+    load = pltpu.make_async_copy(w_out_ref, w_out, load_sem)
+    load.start()
+    greet(me, count, kv, kv_count)
 
     def messages(distance):
         owner = flip(me, distance)
@@ -171,19 +352,20 @@
             for copy in messages(message):
                 copy.wait_recv()
         levels = [lse_ref[owner]] + [got_lse[message] for message in incoming]
+        if not distance:
+            levels.append(tree_lse_ref[...])
         top = functools.reduce(jnp.maximum, levels)
         shares = [jnp.exp(level - top) for level in levels]
         total = functools.reduce(jnp.add, shares)
         inverse = 1.0 / total
         shares = [share * inverse for share in shares]
-        new_lse = top + jnp.log(total)
         if distance:
-            held_lse[distance // 2] = new_lse
-        else:
-            out_lse_ref[...] = new_lse
+            held_lse[distance // 2] = top + jnp.log(total)
         for head in range(heads):
             cols = slice(head * 128, (head + 1) * 128)
             pieces = [part_ref[owner, :, cols]] + [got[message, :, cols] for message in incoming]
+            if not distance:
+                pieces.append(tree_ref[:, cols])
             mixed = functools.reduce(
                 jnp.add,
                 [
@@ -194,39 +376,69 @@
             if distance:
                 held[distance // 2, :, cols] = mixed.astype(held.dtype)
             else:
-                out_ref[:, cols] = mixed
+                attended[:, cols] = (mixed * gate_ref[:, head : head + 1]).astype(jnp.bfloat16)
         if distance:
             send(distance)
+    load.wait()
+    width = out_ref.shape[1]
+
+    def projected(target):
+        cols = pl.ds(pl.multiple_of(target * width, 128), width)
+        return jnp.dot(attended[...], w_out[:, cols], preferred_element_type=jnp.float32)
+
+    def out_message(hop):
+        return pltpu.make_async_remote_copy(
+            src_ref=outgoing.at[hop],
+            dst_ref=arrived.at[hop],
+            send_sem=out_send.at[hop],
+            recv_sem=out_recv.at[hop],
+            device_id={"kv": (kv + hop) % kv_count},
+        )
+
+    for hop in range(1, kv_count):
+        outgoing[hop] = projected((kv + hop) % kv_count).astype(jnp.bfloat16)
+        copy = out_message(hop)
+        copy.start()
+        sent.append(copy)
+    total = projected(kv)
+    for hop in range(1, kv_count):
+        out_message(hop).wait_recv()
+        total = total + arrived[hop].astype(jnp.float32)
+    out_ref[...] = (total + hidden_ref[...].astype(jnp.float32)).astype(jnp.bfloat16)
     for copy in sent:
         copy.wait_send()
 
 
-def merge_parts(parts, lse, count):
+def merge_parts(parts, lse, tree_mix, tree_lse, gate, w_out, hidden, count, kv_count):
     rows, width = parts.shape[1:]
     lanes = lse.shape[2]
     half = max(1, count // 2)
     vmem = pl.BlockSpec(memory_space=pltpu.VMEM)
     return pl.pallas_call(
-        functools.partial(merge_kernel, count),
-        out_shape=(
-            jax.ShapeDtypeStruct((rows, width), jnp.float32),
-            jax.ShapeDtypeStruct((rows, lanes), jnp.float32),
-        ),
-        in_specs=[vmem, vmem],
-        out_specs=(vmem, vmem),
+        functools.partial(merge_kernel, count, kv_count),
+        out_shape=jax.ShapeDtypeStruct(hidden.shape, jnp.bfloat16),
+        in_specs=[vmem] * 5 + [pl.BlockSpec(memory_space=pl.ANY), vmem],
+        out_specs=vmem,
         scratch_shapes=[
             pltpu.VMEM((count, rows, width), parts.dtype),
             pltpu.VMEM((count, rows, lanes), jnp.float32),
             pltpu.VMEM((half, rows, width), parts.dtype),
             pltpu.VMEM((half, rows, lanes), jnp.float32),
+            pltpu.VMEM(w_out.shape, w_out.dtype),
+            pltpu.VMEM((rows, width), jnp.bfloat16),
+            pltpu.VMEM((kv_count,) + hidden.shape, jnp.bfloat16),
+            pltpu.VMEM((kv_count,) + hidden.shape, jnp.bfloat16),
             pltpu.SemaphoreType.DMA((2, count)),
             pltpu.SemaphoreType.DMA((2, count)),
+            pltpu.SemaphoreType.DMA,
+            pltpu.SemaphoreType.DMA((kv_count,)),
+            pltpu.SemaphoreType.DMA((kv_count,)),
         ],
         compiler_params=pltpu.CompilerParams(
             collective_id=1, has_side_effects=True, vmem_limit_bytes=48 * 2**20
         ),
         name="merge_parts",
-    )(parts, lse)
+    )(parts, lse, tree_mix, tree_lse, gate, w_out, hidden)
 
 
 def pool_kernel(
@@ -359,8 +571,8 @@
     pool_dev = cache_keys.shape[0]
     seq_index = lax.axis_index("seq")
     score_scale = 1.0 / math.sqrt(head_width)
-    full_rows = lax.all_gather(hidden, "kv", axis=1, tiled=True)
-    normed = rms_scale(full_rows.astype(jnp.float32), in_gain).astype(jnp.bfloat16)
+    seq_count = requests // local_req
+    kv_count = in_gain.shape[0] // hidden.shape[1]
     reach, depth_f = tree_paths(parents)
     all_reqs = jnp.arange(requests, dtype=jnp.int32)
     my_reqs = seq_index * local_req + jnp.arange(local_req, dtype=jnp.int32)
@@ -372,42 +584,28 @@
         my_pick * own_len[None, :], axis=1
     )
     positions = (context[:, None].astype(jnp.float32) + depth_f).reshape(-1)
-    query = jnp.dot(normed, w_query, preferred_element_type=jnp.float32).reshape(
-        local_tok, local_heads, head_width
-    )
-    query = rotate_pairs(rms_scale(query, q_gain), positions).astype(jnp.bfloat16)
-    key_new = jnp.dot(normed, key_projection_weight, preferred_element_type=jnp.float32).reshape(
-        local_tok, local_kv, head_width
-    )
-    key_new = rotate_pairs(rms_scale(key_new, k_gain), positions).astype(jnp.bfloat16)
-    value_new = (
-        jnp.dot(normed, value_projection_weight, preferred_element_type=jnp.float32)
-        .astype(jnp.bfloat16)
-        .reshape(local_tok, local_kv, head_width)
-    )
-    gate_logit = jnp.dot(normed, w_gate, preferred_element_type=jnp.float32)
-    tree_query = query.reshape(local_req, tree, local_kv, per_kv, head_width)
-    tree_keys = key_new.reshape(local_req, tree, local_kv, head_width)
-    tree_values = value_new.reshape(local_req, tree, local_kv, head_width)
-    tree_scores = (
-        jnp.einsum("atkgd,askd->atkgs", tree_query, tree_keys, preferred_element_type=jnp.float32)
-        * score_scale
-    )
-    tree_seen = (reach > 0.5)[:, :, None, None, :]
-    tree_scores = jnp.where(tree_seen, tree_scores, NEGATIVE)
-    tree_max = jnp.max(tree_scores, axis=-1)
-    tree_weights = jnp.where(tree_seen, jnp.exp(tree_scores - tree_max[..., None]), 0.0)
-    tree_sum = jnp.sum(tree_weights, axis=-1).reshape(local_tok, local_heads)
-    tree_num = jnp.einsum(
-        "atkgs,askd->atkgd",
-        tree_weights.astype(jnp.bfloat16),
-        tree_values,
-        preferred_element_type=jnp.float32,
-    ).reshape(local_tok, local_heads, head_width)
-    tree_max = tree_max.reshape(local_tok, local_heads)
+    cosine, sine = rope_tables(positions, head_width)
+    seen = (reach[:, :, None, :] * jnp.eye(local_req, dtype=jnp.float32)[:, None, :, None]).reshape(
+        local_tok, local_tok
+    )
+    gathered, key_new, value_new, tree_mix, tree_lse, gate = layer_front(
+        hidden,
+        in_gain,
+        w_query,
+        key_projection_weight,
+        value_projection_weight,
+        w_gate,
+        q_gain,
+        k_gain,
+        cosine,
+        sine,
+        seen,
+        seq_count,
+        kv_count,
+        score_scale,
+    )
     lengths_all = jnp.concatenate([prefix_len, own_len])
     starts = jnp.cumsum(lengths_all) - lengths_all
-    seq_count = requests // local_req
     first = jnp.clip(starts - seq_index * pool_dev, 0, pool_dev)
     last = jnp.clip(starts + lengths_all - seq_index * pool_dev, 0, pool_dev)
     same = (request_group[:, None] == request_group[None, :]) & (all_reqs[None, :] < all_reqs[:, None])
@@ -415,7 +613,6 @@
     members = jnp.sum(
         (place[None, :] == all_reqs[:, None]).astype(jnp.int32) * all_reqs[None, :], axis=1
     )
-    gathered = gather_rows(query.reshape(local_tok, local_heads * head_width), seq_count)
     parts, part_lse = pool_attention(
         first,
         last,
@@ -427,31 +624,17 @@
         per_kv,
         score_scale,
     )
-    cache_mix, cache_lse = merge_parts(
+    layer_out = merge_parts(
         parts.reshape(seq_count, local_tok, local_heads * head_width),
         part_lse.reshape(seq_count, local_tok, 128),
+        tree_mix,
+        tree_lse,
+        gate,
+        w_out,
+        hidden,
         seq_count,
-    )
-    cache_lse = cache_lse[:, :local_heads]
-    final_max = jnp.maximum(cache_lse, tree_max)
-    cache_factor = jnp.exp(cache_lse - final_max)
-    tree_factor = jnp.exp(tree_max - final_max)
-    weight_sum = cache_factor + tree_sum * tree_factor
-    mixed = (
-        cache_mix.reshape(local_tok, local_heads, head_width) * cache_factor[..., None]
-        + tree_num * tree_factor[..., None]
-    )
-    mixed = mixed / weight_sum[..., None]
-    attended = (
-        (mixed * jax.nn.sigmoid(gate_logit)[..., None])
-        .astype(jnp.bfloat16)
-        .reshape(local_tok, local_heads * head_width)
-    )
-    projected = jnp.dot(attended, w_out, preferred_element_type=jnp.float32)
-    layer_part = lax.psum_scatter(
-        projected.astype(jnp.bfloat16), "kv", scatter_dimension=1, tiled=True
-    ).astype(jnp.float32)
-    layer_out = (layer_part + hidden.astype(jnp.float32)).astype(jnp.bfloat16)
+        kv_count,
+    )
     tree_rows = jnp.concatenate(
         [
             key_new.reshape(local_req, tree, local_kv * head_width),

time: 138 us -> 95.5 us (0.69); the launches traced: 136 us -> 95.1 us
  between operations: 14.7 us -> 0.78 us
  Pallas kernels: 62.6 us -> 76 us
  waiting for transfers between devices: 10.8 us -> 0 us
  matrix products: 12.1 us -> 2.18 us
  local copies, waits for them, and re-layouts: 18.4 us -> 9.88 us
  blocking collectives: 7.5 us -> 0 us
  other arithmetic: 9.86 us -> 6.3 us
    pallas_call x2, Pallas kernels: 47.3 us -> 61 us  [the longest x1 32.9 us: merge_parts(): pl.pallas_call(functools.partial(merge_kernel, count, kv_count), out_shap...]
    reduce_scatter x1 -> x0, waiting for transfers between devices: 10.8 us -> none  [body(): lax.psum_scatter(projected.astype(jnp.bfloat16), 'kv', scatter_dimension=...]
    dot_general x7 -> x0, matrix products: 10.7 us -> none  [the longest x1 3.12 us: body(): jnp.dot(normed, w_query, preferred_element_type=jnp.float32)]
    all_gather x1 -> x0, blocking collectives: 7.5 us -> none  [body(): full_rows = lax.all_gather(hidden, 'kv', axis=1, tiled=True)]
    unnamed x59 -> x16, local copies, waits for them, and re-layouts: 0.98 us -> 6.19 us
    reshape x8 -> x0, local copies, waits for them, and re-layouts: 4.87 us -> none  [the longest x2 2.13 us: body(): tree_max = tree_max.reshape(local_tok, local_heads)]
    mul x13 -> x1, local copies, waits for them, and re-layouts: 3.5 us -> 0.1 us  [body(): reach[:, :, None, :]]
    convert_element_type x3 -> x1, other arithmetic: 2.59 us -> 0.01 us  [body(): jnp.eye(local_req, dtype=jnp.float32)[:, None, :, None]]
  transfers between devices with their start and end apart: 1 -> 0, of which waited for: 1 -> 0; matrix products, arithmetic and copies ran while one was open for 1% -> 0% of each run, Pallas kernels for 0% -> 0%
where the time goes in v2:
time: 95.5 us; the launch traced here: 95.1 us
  Pallas kernels  76 us (80%)
  local copies, waits for them, and re-layouts  9.88 us (10%)
  other arithmetic  6.3 us (7%)
  matrix products  2.18 us (2%)
    pallas_call x1, Pallas kernels, merge_parts(): pl.pallas_call(functools.partial(merge_kernel, count, kv_count), out_shap...  32.9 us
    pallas_call x1, Pallas kernels, layer_front(): pl.pallas_call(functools.partial(layer_kernel, count, kv_count, score_sca...  28.1 us
    pallas_call x1, Pallas kernels, pool_attention(): pl.pallas_call(functools.partial(pool_kernel, groups, per_kv, min(512, ke...  15 us
    unnamed x16, local copies, waits for them, and re-layouts  6.19 us
    reshape x1, local copies, waits for them, and re-layouts, body(): pooled_cache_values.reshape(pool_dev, local_kv * head_width)  2.74 us

profile of v2, /device:TPU:0, one launch (start us, length us, event | category | flops | bytes accessed | tf_op | source)
XLA Modules:
  0.0 95.1 jit_solution(2123200947160894357)
XLA Ops:
  0.6 0.7 compare_bitcast_fusion
  1.4 0.7 fusion.27
  2.1 0.9 convert_reduce_fusion
  3.0 0.7 multiply_add_fusion
  3.7 0.1 select_reduce_fusion.member_ref
  3.8 0.9 select_reduce_fusion.1
  4.7 0.8 fusion.22
  5.6 1.0 %convolution_minimum_fusion.4 = f32[2,32,32]{2,1,0:T(8,128)S(1)} fusion(f32[32,32]{1,0:T(8,128)S(1)} %broadcast_subtract_fusion, s32[2,32]{1,0:T(2,128)} %param.30, f32[32,32]{1,0:T(8,128)S(1)} %fusion.18), kind=kOutput, calls=%fused_computation.7 | convolution fusion | flops 796672 | bytes 16640 | tf_op jit(solution)/shard_map/mij,mjk->mik/dot_general | solution.py:43
  6.6 0.2 convolution_minimum_fusion.3
  6.8 0.2 convolution_minimum_fusion.2
  6.9 0.2 convolution_minimum_fusion.1
  7.1 0.2 fusion.29
  7.4 0.1 fusion.20
  7.5 0.1 broadcast_add_fusion
  7.6 0.1 add.62
  7.7 0.1 copy.29
  7.8 0.1 reduce-window.9
  7.8 0.1 reduce
  7.9 0.8 subtract_clamp_fusion
  8.7 0.1 broadcast_multiply_fusion
  8.8 0.1 mul.120.seen_ref
  8.9 0.2 fusion.19
  9.1 0.1 pad_maximum_fusion
  9.2 1.0 %copy.32.w_gate_ref = bf16[2048,8]{1,0:T(8,128)(2,1)S(1)} copy(bf16[2048,8]{0,1:T(8,128)(2,1)} %param.21) | data formatting | bytes 65536 | tf_op args[5]
  10.2 0.0 copy-start
  10.2 1.6 %copy-done = bf16[2048,512]{1,0:T(8,128)(2,1)S(1)} copy-done((bf16[2048,512]{1,0:T(8,128)(2,1)S(1)}, bf16[2048,512]{1,0:T(8,128)(2,1)}, u32[]{:S(2)}) %copy-start) | copy-done | bytes 2097176
  11.8 0.0 copy-start.1
  11.8 0.9 copy-done.1
  12.7 0.0 copy-start.2
  12.7 0.7 copy-done.2
  13.4 0.0 copy-start.3
  13.4 0.7 copy-done.3
  14.1 0.0 copy-start.4
  14.1 0.7 copy-done.4
  14.7 0.0 copy-start.5
  14.7 0.0 copy-start.6
  14.7 28.1 %layer_front.1 = (bf16[16,64,1024]{2,1,0:T(8,128)(2,1)S(1)}, bf16[64,512]{1,0:T(8,128)(2,1)S(1)}, bf16[64,512]{1,0:T(8,128)(2,1)S(1)}, f32[64,1024]{1,0:T(8,128)...) custom-call(bf16[64,1024]{1,0:T(8,128)(2,1)S(1)} %copy-done.1, f32[1,2048]{1,0:T(1,128)S(1)} %bitcast.34, ...), custom_call_target="tpu_custom_call" | custom-call | tf_op jit(solution)/shard_map/layer_front/pallas_call | solution.py:259
  42.9 0.3 convolution_convert_fusion
  43.2 0.7 fusion.28
  43.9 0.0 copy-done.5
  43.9 0.0 copy-done.6
  43.9 2.7 %copy_bitcast_fusion = (bf16[2048,512]{1,0:T(8,128)(2,1)}, bf16[2048,512]{1,0:T(8,128)(2,1)}) fusion(bf16[256,8,4,128]{3,2,1,0:T(4,128)(2,1)S(1)} %bitcast.37, bf16[256,8,4,128]{3,2,1,0:T(4,128)(2,1)S(1)} %bitcast.38), kind=kLoop, calls=%fused_computation | loop fusion | bytes 8388608 | tf_op jit(solution)/shard_map/reshape | solution.py:622
  46.6 15.0 %pool_attention.1 = (bf16[32,32,1024]{2,1,0:T(8,128)(2,1)S(1)}, f32[32,32,128]{2,1,0:T(8,128)S(1)}) custom-call(s32[36]{0:T(128)S(1)} %get-tuple-element.29.first_ref, s32[36]{0:T(128)S(1)} %get-tuple-element.28.last_ref, s32[32]{0:T(128)S(1)} %select_reduce_fusion.member_ref, bf16[32,32,1024]{2,1,0:T(8,128)(2,1)S(1)} %bitcast.30, ...), custom_call_target="tpu_custom_call" | custom-call | tf_op jit(solution)/shard_map/pool_attention/pallas_call | solution.py:532
  61.6 32.9 %merge_parts.1 = bf16[64,1024]{1,0:T(8,128)(2,1)S(1)} custom-call(bf16[16,64,1024]{2,1,0:T(8,128)(2,1)S(1)} %bitcast.29, f32[16,64,128]{2,1,0:T(8,128)S(1)} %bitcast.31, f32[64,1024]{1,0:T(8,128)S(1)} %get-tuple-element.14.tree_ref, f32[64,128]{1,0:T(8,128)S(1)} %get-tuple-element.15.tree_lse_ref, f32[64,8]{1,0:T(8,128)S(1)} %get-tuple-element.16.gate_ref, ...), custom_call_target="tpu_custom_call" | custom-call | tf_op jit(solution)/shard_map/merge_parts/pallas_call | solution.py:417
  94.5 0.7 copy.44
  (7 shorter events, 0.0 us)
Async XLA Ops:
  10.2 1.6 %copy-start = (bf16[2048,512]{1,0:T(8,128)(2,1)S(1)}, bf16[2048,512]{1,0:T(8,128)(2,1)}, u32[]{:S(2)}) copy-start(bf16[2048,512]{1,0:T(8,128)(2,1)} %w_key_ref.1) | copy-start | bytes 6291460
  11.8 0.9 copy-start.1
  12.7 0.7 copy-start.2
  13.4 0.7 copy-start.3
  14.1 0.7 copy-start.4
  14.7 29.1 %copy-start.5 = (bf16[2048,4,128]{2,1,0:T(4,128)(2,1)S(1)}, bf16[2048,4,128]{2,1,0:T(4,128)(2,1)}, u32[]{:S(2)}) copy-start(bf16[2048,4,128]{2,1,0:T(4,128)(2,1)} %param.26) | copy-start | bytes 6291460
  14.7 29.1 %copy-start.6 = (bf16[2048,4,128]{2,1,0:T(4,128)(2,1)S(1)}, bf16[2048,4,128]{2,1,0:T(4,128)(2,1)}, u32[]{:S(2)}) copy-start(bf16[2048,4,128]{2,1,0:T(4,128)(2,1)} %param.25) | copy-start | bytes 6291460
